TPU v7x, 32 devices: a whole 2x2x4 slice. The times are simulated.
32 devices in a mesh: groups: 2 (over x), seq: 16 (over z, y, core).
Axes of the slice: x: 2, y: 2, z: 4, core: 2. Of those that a mesh axis runs over, the one named last changes fastest.
Arguments:
- queries: bfloat16 [256, 2560], P(('groups', 'seq')), parts along dimension 0, may hold values from -130 to 130
- cache_keys: bfloat16 [32768, 2560], P(('groups', 'seq')), parts along dimension 0, may hold values from -6 to 6
- cache_values: bfloat16 [32768, 2560], P(('groups', 'seq')), parts along dimension 0, may hold values from -6 to 6
- span_keys: bfloat16 [256, 2560], P(('groups', 'seq')), parts along dimension 0, may hold values from -8 to 8
- span_values: bfloat16 [256, 2560], P(('groups', 'seq')), parts along dimension 0, may hold values from -6 to 6
- cache_tokens: int32 [2], P('groups'), parts along dimension 0, may hold values from 8192 to 16384
- span_start: int32 [2], P('groups'), parts along dimension 0, may hold values from 1433 to 1559
Outputs:
- attended: bfloat16 [256, 2560], P(('groups', 'seq')), parts along dimension 0
There are 2 independent parts, one for each index of `groups`. A program takes and returns all parts, laid end to end along the dimension named above; each array names one. Nothing has to cross between parts.
All inputs are finite; a program needn't handle non-finite values.
Results may differ from a plain program's by a relative error of at most 0.0026.
Values may be sent and summed in bfloat16 or wider, within the bound.
No kernel may reach another device: no remote copies, remote signals or barrier semaphores. Data moves between devices by JAX's collectives and lax.ppermute only.
A program may use at most 320 MiB of HBM per device.

v0:
```python
import math

import jax
import jax.numpy as jnp
from jax import lax
from jax.sharding import PartitionSpec as P

HEAD_DIM = 128
HEADS = 20
FRAME_TOK = 1560


NEG_FILL = -1e30


def local(queries, cache_keys, cache_values, span_keys, span_values, cache_tokens, span_start):
    device_index = lax.axis_index("seq")
    cache_rows = cache_keys.shape[0]
    own_tokens = queries.shape[0]
    score_scale = 1.0 / math.sqrt(HEAD_DIM)
    valid_end = cache_tokens[0]
    frame_offset = span_start[0]
    all_queries = lax.all_gather(queries, "seq", axis=0, tiled=True)
    total_rows = all_queries.shape[0]
    query_heads = all_queries.reshape(total_rows, HEADS, HEAD_DIM)
    slot_ids = jnp.arange(cache_rows, dtype=jnp.int32)
    key_rows, value_rows = (cache_keys, cache_values)
    position = device_index * cache_rows + slot_ids
    used_rows = jnp.clip(valid_end - device_index * cache_rows, 0, cache_rows)
    key_rows = key_rows.reshape(cache_rows, HEADS, HEAD_DIM)
    value_rows = value_rows.reshape(cache_rows, HEADS, HEAD_DIM)
    block_rows = min(512, cache_rows)
    block_total = cache_rows // block_rows
    block_count = (used_rows + block_rows - 1) // block_rows
    query_frame = (frame_offset + jnp.arange(total_rows, dtype=jnp.int32)) // FRAME_TOK
    key_frame = (
        frame_offset + device_index * own_tokens + jnp.arange(own_tokens, dtype=jnp.int32)
    ) // FRAME_TOK
    own_keys = span_keys.reshape(own_tokens, HEADS, HEAD_DIM)
    own_values = span_values.reshape(own_tokens, HEADS, HEAD_DIM)
    span_scores = (
        jnp.einsum("qhd,khd->hqk", query_heads, own_keys, preferred_element_type=jnp.float32)
        * score_scale
    )
    span_scores = jnp.where(
        (key_frame[None, :] <= query_frame[:, None])[None], span_scores, NEG_FILL
    )

    def block_scores(step_index):
        begin = step_index * block_rows
        key_piece = lax.dynamic_slice_in_dim(key_rows, begin, block_rows, 0)
        scores = (
            jnp.einsum("qhd,khd->hqk", query_heads, key_piece, preferred_element_type=jnp.float32)
            * score_scale
        )
        spot = lax.dynamic_slice_in_dim(position, begin, block_rows, 0)
        return jnp.where((spot < valid_end)[None, None, :], scores, NEG_FILL)

    def store_step(step_index, stored):
        return lax.dynamic_update_index_in_dim(stored, block_scores(step_index), step_index, 0)

    empty_store = jnp.full((block_total, HEADS, total_rows, block_rows), NEG_FILL, jnp.float32)
    stored = lax.fori_loop(0, block_count, store_step, empty_store)
    local_top = jnp.maximum(jnp.max(span_scores, axis=2), jnp.max(stored, axis=(0, 3)))
    row_top = lax.pmax(local_top, "seq")

    def weigh(scores, value_piece):
        weights = jnp.exp(scores - row_top[:, :, None])
        rounded = weights.astype(jnp.bfloat16)
        numer = jnp.einsum("hqk,khd->qhd", rounded, value_piece, preferred_element_type=jnp.float32)
        return (jnp.sum(weights, axis=2), numer)

    first_den, first_num = weigh(span_scores, own_values)

    def sum_step(step_index, running):
        value_piece = lax.dynamic_slice_in_dim(value_rows, step_index * block_rows, block_rows, 0)
        scores = lax.dynamic_index_in_dim(stored, step_index, 0, keepdims=False)
        part_den, part_num = weigh(scores, value_piece)
        return (running[0] + part_den, running[1] + part_num)

    denominator, numerator = lax.fori_loop(0, block_count, sum_step, (first_den, first_num))
    numerator = numerator.reshape(total_rows, HEADS * HEAD_DIM)
    mine_num, mine_den = (
        lax.psum_scatter(numerator, "seq", scatter_dimension=0, tiled=True),
        lax.psum_scatter(denominator, "seq", scatter_dimension=1, tiled=True),
    )
    attended = mine_num.reshape(own_tokens, HEADS, HEAD_DIM) / jnp.transpose(mine_den)[:, :, None]
    return attended.reshape(own_tokens, HEADS * HEAD_DIM).astype(jnp.bfloat16)


def solution(mesh):
    placed = (
        P(("groups", "seq"), None),
        P(("groups", "seq"), None),
        P(("groups", "seq"), None),
        P(("groups", "seq"), None),
        P(("groups", "seq"), None),
        P("groups"),
        P("groups"),
    )
    return jax.shard_map(
        local, mesh=mesh, in_specs=placed, out_specs=P(("groups", "seq"), None), check_vma=False
    )
```

profile of v0, /device:TPU:0, one launch (start us, length us, event | category | flops | bytes accessed | tf_op | source)
XLA Modules:
  0.0 235.5 jit_solution(13375473434348146988)
XLA Ops:
  6.5 0.0 copy-start
  6.5 0.0 reduce-scatter.5.cloned.1.call-start
  7.2 25.4 %all_gather.3 = bf16[128,2560]{1,0:T(8,128)(2,1)S(1)} all-gather(bf16[8,2560]{1,0:T(8,128)(2,1)} %param.11), channel_id=1, replica_groups=mesh['groups'=2,'seq'=16] {'seq'}, dimensions={0}, use_global_device_ids=true | all-gather | bytes 696320 | tf_op jit(solution)/shard_map/all_gather | solution.py:23
  32.6 0.3 copy.21
  32.9 0.4 copy.25
  33.3 8.0 %copy.23 = bf16[1024,2560]{0,1:T(8,128)(2,1)} copy(bf16[1024,2560]{1,0:T(8,128)(2,1)} %param.12) | data formatting | bytes 10485760 | tf_op args[1]
  41.3 5.2 %broadcast_in_dim.40 = f32[2,20,128,512]{2,3,1,0:T(8,128)} broadcast(f32[]{:T(128)} %constant.76.clone.1), dimensions={} | broadcast | bytes 10485764 | tf_op jit(solution)/shard_map/broadcast_in_dim | solution.py:62
  46.5 12.3 %while.22 = (s32[]{:T(128)}, f32[2,20,128,512]{2,3,1,0:T(8,128)}, s32[]{:T(128)}, s32[1024]{0:T(1024)S(1)}, s32[]{:T(128)}, /*index=5*/bf16[1024,20,128]{0,2,1:T...) while((s32[]{:T(128)}, f32[2,20,128,512]{2,3,1,0:T(8,128)}, ...), condition=%wide.region_2.3_spmd, body=%wide.region_1.2_spmd.sunk | while | flops 338166272 | bytes 8522965 | solution.py:63
  46.5 0.7 dynamic-slice_compare_fusion.2
  47.2 5.4 %bitcast_dynamic-update-slice_fusion.2 = f32[2,20,128,512]{2,3,1,0:T(8,128)} fusion(f32[2,20,128,512]{2,3,1,0:T(8,128)} %get-tuple-element.251, s32[]{:T(128)S(6)} %select_n.63, pred[512]{0:T(512)(128)(4,1)S(1)} %dynamic-slice_compare_fusion.2, bf16[128,20,128]{2,0,1:T(8,128)(2,1)S(1)} %get-tuple-element.268, ...), kind=kOutput, calls=%fused_computation.clone.1 | convolution fusion | flops 338165760 | bytes 8520200 | tf_op jit(solution)/shard_map/while/body/qhd,khd->hqk/dot_general | solution.py:53
  52.6 0.7 dynamic-slice_compare_fusion.2
  53.3 5.4 %bitcast_dynamic-update-slice_fusion.2 = f32[2,20,128,512]{2,3,1,0:T(8,128)} fusion(f32[2,20,128,512]{2,3,1,0:T(8,128)} %get-tuple-element.251, s32[]{:T(128)S(6)} %select_n.63, pred[512]{0:T(512)(128)(4,1)S(1)} %dynamic-slice_compare_fusion.2, bf16[128,20,128]{2,0,1:T(8,128)(2,1)S(1)} %get-tuple-element.268, ...), kind=kOutput, calls=%fused_computation.clone.1 | convolution fusion | flops 338165760 | bytes 8520200 | tf_op jit(solution)/shard_map/while/body/qhd,khd->hqk/dot_general | solution.py:53
  59.5 0.0 copy-start.2
  59.5 4.5 %reduce_max.19 = f32[20,128]{1,0:T(8,128)S(1)} reduce(f32[2,20,128,512]{2,3,1,0:T(8,128)} %get-tuple-element.278, f32[]{:T(128)} %constant.77.clone.1), dimensions={0,3}, to_apply=%region_3.4 | reduce | flops 2618880 | bytes 10496004 | tf_op jit(solution)/shard_map/reduce_max | solution.py:64
  64.0 0.1 broadcast_compare_fusion
  64.0 0.0 copy-done.2
  64.1 0.3 fusion.31
  64.4 57.8 %pmax.7 = f32[20,128]{1,0:T(8,128)S(1)} all-reduce(f32[20,128]{1,0:T(8,128)S(1)} %max.10), channel_id=1, replica_groups=mesh['groups'=2,'seq'=16] {'seq'}, use_global_device_ids=true, to_apply=%region_4.5 | all-reduce | flops 2560 | bytes 20480 | tf_op jit(solution)/shard_map/pmax | solution.py:65
  122.2 0.0 copy-done
  122.2 0.4 convolution_bitcast_fusion
  122.7 0.4 copy.27
  123.1 8.0 %copy.26 = bf16[1024,2560]{0,1:T(8,128)(2,1)} copy(bf16[1024,2560]{1,0:T(8,128)(2,1)} %param.13) | data formatting | bytes 10485760 | tf_op args[2]
  131.0 0.0 copy-start.3
  131.0 34.7 %while.23 = (s32[]{:T(128)}, f32[20,128]{1,0:T(8,128)S(1)}, f32[128,20,128]{0,2,1:T(8,128)S(1)}, s32[]{:T(128)}, f32[2,20,128,512]{2,3,1,0:T(8,128)}, /*index=5*...) while((s32[]{:T(128)}, f32[20,128]{1,0:T(8,128)S(1)}, ...), condition=%wide.region_8.9_spmd, body=%wide.region_6.8_spmd.sunk | while | flops 341114880 | bytes 57733352 | solution.py:81
  131.0 5.2 %constant_dynamic-slice_fusion.2 = f32[1,20,128,512]{2,3,1,0:T(8,128)} fusion(f32[2,20,128,512]{2,3,1,0:T(8,128)} %get-tuple-element.302, s32[]{:T(128)S(6)} %select_n.65), kind=kLoop, calls=%fused_computation.15.clone.1 | loop fusion | bytes 10485764 | tf_op jit(solution)/shard_map/while/body/jit(dynamic_index_in_dim)/dynamic_slice | solution.py:77
  136.3 6.0 %copy.38 = f32[1,20,128,512]{3,2,1,0:T(8,128)} copy(f32[1,20,128,512]{2,3,1,0:T(8,128)} %constant_dynamic-slice_fusion.2) | data formatting | bytes 10485760 | tf_op jit(solution)/shard_map/while/body/jit(dynamic_index_in_dim)/dynamic_slice | solution.py:77
  142.2 0.0 copy-start.1
  142.2 4.7 %fusion.45 = f32[128,20,128]{0,2,1:T(8,128)S(1)} fusion(f32[128,20,128]{0,2,1:T(8,128)S(1)} %get-tuple-element.288, f32[1,20,128,512]{3,2,1,0:T(8,128)} %copy.38, f32[20,128]{1,0:T(8,128)S(1)} %get-tuple-element.303, bf16[1024,20,128]{0,2,1:T(8,128)(2,1)} %get-tuple-element.304, s32[]{:T(128)S(6)} %select_n.66), kind=kOutput, calls=%fused_computation.13.clone.1 | convolution fusion | flops 338493440 | bytes 10496004 | tf_op jit(solution)/shard_map/while/body/hqk,khd->qhd/dot_general | solution.py:70
  146.9 0.0 copy-done.1
  147.0 1.4 fusion.44
  148.4 5.2 %constant_dynamic-slice_fusion.2 = f32[1,20,128,512]{2,3,1,0:T(8,128)} fusion(f32[2,20,128,512]{2,3,1,0:T(8,128)} %get-tuple-element.302, s32[]{:T(128)S(6)} %select_n.65), kind=kLoop, calls=%fused_computation.15.clone.1 | loop fusion | bytes 10485764 | tf_op jit(solution)/shard_map/while/body/jit(dynamic_index_in_dim)/dynamic_slice | solution.py:77
  153.6 6.0 %copy.38 = f32[1,20,128,512]{3,2,1,0:T(8,128)} copy(f32[1,20,128,512]{2,3,1,0:T(8,128)} %constant_dynamic-slice_fusion.2) | data formatting | bytes 10485760 | tf_op jit(solution)/shard_map/while/body/jit(dynamic_index_in_dim)/dynamic_slice | solution.py:77
  159.6 0.0 copy-start.1
  159.6 4.7 %fusion.45 = f32[128,20,128]{0,2,1:T(8,128)S(1)} fusion(f32[128,20,128]{0,2,1:T(8,128)S(1)} %get-tuple-element.288, f32[1,20,128,512]{3,2,1,0:T(8,128)} %copy.38, f32[20,128]{1,0:T(8,128)S(1)} %get-tuple-element.303, bf16[1024,20,128]{0,2,1:T(8,128)(2,1)} %get-tuple-element.304, s32[]{:T(128)S(6)} %select_n.66), kind=kOutput, calls=%fused_computation.13.clone.1 | convolution fusion | flops 338493440 | bytes 10496004 | tf_op jit(solution)/shard_map/while/body/hqk,khd->qhd/dot_general | solution.py:70
  164.3 0.0 copy-done.1
  164.4 1.4 fusion.44
  165.7 1.5 copy.31
  167.2 0.0 reduce-scatter.5.cloned.1.call-update
  167.2 0.0 copy-done.3
  167.2 0.6 dynamic-slice
  168.5 57.8 %all-reduce = f32[20,128]{1,0:T(8,128)S(1)} all-reduce(f32[20,128]{1,0:T(8,128)S(1)} %get-tuple-element.84), channel_id=3, replica_groups=mesh['groups'=2,'seq'=16] {'seq'}, use_global_device_ids=true, to_apply=%region_10.11.clone | all-reduce | flops 2560 | bytes 20480
  226.3 0.1 dynamic-slice_bitcast_fusion
  226.4 0.0 reduce-scatter.5.cloned.1.call-done
  226.4 1.3 copy.32
  227.7 0.1 fusion.23
  227.8 0.9 copy.29
  (7 shorter events, 0.1 us)
Async XLA Ops:
  6.5 115.7 %copy-start = (bf16[8,2560]{1,0:T(8,128)(2,1)S(1)}, bf16[8,2560]{1,0:T(8,128)(2,1)}, u32[]{:S(2)}) copy-start(bf16[8,2560]{1,0:T(8,128)(2,1)} %param.15) | copy-start | bytes 122884
  6.5 219.9 %reduce-scatter.5.cloned.1.call-start = ((), (), s32[]{:S(2)}) async-start(), calls=%async_computation.1 | async-start | bytes 1392640
  59.5 4.6 %copy-start.2 = (bf16[8,2560]{1,0:T(8,128)(2,1)S(1)}, bf16[8,2560]{1,0:T(8,128)(2,1)}, u32[]{:S(2)}) copy-start(bf16[8,2560]{1,0:T(8,128)(2,1)} %param.14) | copy-start | bytes 122884
  131.0 36.2 %copy-start.3 = (u32[32]{0:T(128)S(1)}, u32[32]{0:T(128)}, u32[]{:S(2)}) copy-start(u32[32]{0:T(128)} %constant.89) | copy-start | bytes 388
  142.2 4.8 %copy-start.1 = (f32[1,20,128,512]{3,2,1,0:T(8,128)S(1)}, f32[1,20,128,512]{3,2,1,0:T(8,128)}, u32[]{:S(2)}) copy-start(f32[1,20,128,512]{3,2,1,0:T(8,128)} %copy.38) | copy-start | bytes 15728644 | tf_op jit(solution)/shard_map/while
  159.6 4.8 %copy-start.1 = (f32[1,20,128,512]{3,2,1,0:T(8,128)S(1)}, f32[1,20,128,512]{3,2,1,0:T(8,128)}, u32[]{:S(2)}) copy-start(f32[1,20,128,512]{3,2,1,0:T(8,128)} %copy.38) | copy-start | bytes 15728644 | tf_op jit(solution)/shard_map/while
Sparse Core Ops, SparseCore 0:
  167.3 56.0 reduce-scatter.4
where the time goes:
time: 237 us; the launch traced here: 236 us
  blocking collectives  141 us (59%)
  local copies, waits for them, and re-layouts  49 us (21%)
  matrix products  21 us (9%)
  between operations  15.5 us (7%)
  other arithmetic  8.89 us (4%)
    unnamed x1, blocking collectives  57.8 us
    pmax x1, blocking collectives, local(): row_top = lax.pmax(local_top, 'seq')  57.8 us
    all_gather x1, blocking collectives, local(): all_queries = lax.all_gather(queries, 'seq', axis=0, tiled=True)  25.4 us
    dynamic_slice x4, local copies, waits for them, and re-layouts, sum_step(): scores = lax.dynamic_index_in_dim(stored, step_index, 0, keepdims=False)  22.4 us
    unnamed x11, local copies, waits for them, and re-layouts  19.3 us
    dot_general x2, matrix products, block_scores(): jnp.einsum('qhd,khd->hqk', query_heads, key_piece, preferred_element_type...  10.9 us
    dot_general x3, matrix products, weigh(): jnp.einsum('hqk,khd->qhd', rounded, value_piece, preferred_element_type=j...  9.83 us
    broadcast_in_dim x1, local copies, waits for them, and re-layouts, local(): jnp.full((block_total, HEADS, total_rows, block_rows), NEG_FILL, jnp.floa...  5.23 us
  transfers between devices with their start and end apart: 1, of which 0 were waited for; matrix products, arithmetic and copies ran while one was open for 0% of the time, Pallas kernels for 0%

commit v1 on v0

v1 whole, which is shorter than its diff:
```python
import functools
import math

import jax
import jax.numpy as jnp
from jax import lax
from jax.experimental import pallas as pl
from jax.experimental.pallas import tpu as pltpu
from jax.sharding import PartitionSpec as P

HEAD_DIM = 128
HEADS = 20
FRAME_TOK = 1560
LANES = 128
PART = 32
NEG_FILL = -1e30
LOG_FLOOR = -30000.0
FIXED = 32768.0
HALF_RANGE = 32768
STEPS = 32512.0
PEAK_FLOOR = 1e-30
SCALE = math.log2(math.e) / math.sqrt(HEAD_DIM)
WIDTH = HEADS * HEAD_DIM
PER_STEP = 2


def pack(o):
    peak = jnp.max(jnp.abs(o), axis=1, keepdims=True)
    power = jnp.ceil(jnp.log2(jnp.maximum(peak, PEAK_FLOOR)))
    steps = jnp.round(o * (jnp.exp2(-power) * STEPS))
    return steps.astype(jnp.int32).astype(jnp.int16), power


def unpack(steps):
    return steps.astype(jnp.int32).astype(jnp.float32)


def pack_stats(log_sum, power):
    fixed = jnp.round(log_sum * FIXED).astype(jnp.int32)
    high = fixed // HALF_RANGE
    low = fixed - high * HALF_RANGE
    lane = lax.broadcasted_iota(jnp.int32, log_sum.shape, 1)
    packed = jnp.where(lane < PART, high, pltpu.roll(low, PART, 1))
    packed = jnp.where(lane < 2 * PART, packed, pltpu.roll(power.astype(jnp.int32), 2 * PART, 1))
    return packed.astype(jnp.int16)


def unpack_stats(packed):
    packed = packed.astype(jnp.int32)
    fixed = packed * HALF_RANGE + pltpu.roll(packed, LANES - PART, 1)
    power = pltpu.roll(packed, LANES - 2 * PART, 1)
    return fixed.astype(jnp.float32) * (1.0 / FIXED), power.astype(jnp.float32)


def attend_kernel(limit_ref, q_ref, k_ref, v_ref, sk_ref, sv_ref, qf_ref, kf_ref, keep_ref, keep_log_ref, send_ref, send_log_ref, logs, powers):
    step = pl.program_id(0)
    rows, keys = q_ref.shape[0], k_ref.shape[0]
    half = rows // 2
    used = limit_ref[0]
    slot = lax.broadcasted_iota(jnp.int32, (1, keys), 1)
    bias = jnp.where(slot < used, 0.0, NEG_FILL)
    span_bias = jnp.where(kf_ref[0:1, :] <= qf_ref[:, 0:1], 0.0, NEG_FILL)
    contract_last = (((1,), (1,)), ((), ()))
    @pl.when(step == 0)
    def _():
        logs[...] = jnp.zeros_like(logs)
        powers[...] = jnp.zeros_like(powers)

    for part in range(PER_STEP):
        cols = slice(part * HEAD_DIM, (part + 1) * HEAD_DIM)
        q = q_ref[:, cols]
        s = lax.dot_general(q, k_ref[:, cols], contract_last, preferred_element_type=jnp.float32) + bias
        s2 = lax.dot_general(q, sk_ref[:, cols], contract_last, preferred_element_type=jnp.float32) + span_bias
        top = jnp.maximum(jnp.max(s, axis=1, keepdims=True), jnp.max(s2, axis=1, keepdims=True))
        p = jnp.exp2((s - top) * SCALE)
        p2 = jnp.exp2((s2 - top) * SCALE)
        total = jnp.sum(p, axis=1, keepdims=True) + jnp.sum(p2, axis=1, keepdims=True)
        high = p.astype(jnp.bfloat16)
        low = (p - high.astype(jnp.float32)).astype(jnp.bfloat16)
        v = v_ref[:, cols]
        o = jnp.dot(high, v, preferred_element_type=jnp.float32) + jnp.dot(low, v, preferred_element_type=jnp.float32)
        high2 = p2.astype(jnp.bfloat16)
        low2 = (p2 - high2.astype(jnp.float32)).astype(jnp.bfloat16)
        sv = sv_ref[:, cols]
        o = o + jnp.dot(high2, sv, preferred_element_type=jnp.float32) + jnp.dot(low2, sv, preferred_element_type=jnp.float32)
        o = o * (1.0 / total)
        log_sum = jnp.maximum(top * SCALE + jnp.log2(total), LOG_FLOOR)
        keep_ref[:, cols] = o[:half]
        send_ref[:, cols], power = pack(o[half:])
        lane = lax.broadcasted_iota(jnp.int32, (rows, LANES), 1)
        logs[...] = jnp.where(lane == step * PER_STEP + part, log_sum, logs[...])
        powers[...] = jnp.where(lane[half:] == step * PER_STEP + part, power, powers[...])

    @pl.when(step == pl.num_programs(0) - 1)
    def _():
        keep_log_ref[...] = logs[:half, :]
        send_log_ref[...] = pack_stats(logs[half:, :], powers[...])


def attend(limit, q, k, v, sk, sv, query_frame, key_frame):
    rows, keys, own = q.shape[0], k.shape[0], sk.shape[0]
    half = rows // 2
    block = PER_STEP * HEAD_DIM
    column = lambda n: pl.BlockSpec((n, block), lambda i, *_: (0, i))
    whole = lambda shape: pl.BlockSpec(shape, lambda i, *_: (0, 0))
    return pl.pallas_call(
        attend_kernel,
        grid_spec=pltpu.PrefetchScalarGridSpec(
            num_scalar_prefetch=1,
            grid=(HEADS // PER_STEP,),
            in_specs=[column(rows), column(keys), column(keys), column(own), column(own), whole((rows, LANES)), whole((8, own))],
            out_specs=[column(half), whole((half, LANES)), column(half), whole((half, LANES))],
            scratch_shapes=[pltpu.VMEM((rows, LANES), jnp.float32), pltpu.VMEM((half, LANES), jnp.float32)],
        ),
        out_shape=[
            jax.ShapeDtypeStruct((half, WIDTH), jnp.float32),
            jax.ShapeDtypeStruct((half, LANES), jnp.float32),
            jax.ShapeDtypeStruct((half, WIDTH), jnp.int16),
            jax.ShapeDtypeStruct((half, LANES), jnp.int16),
        ],
        compiler_params=pltpu.CompilerParams(vmem_limit_bytes=24 << 20),
        name="attend",
    )(limit, q, k, v, sk, sv, query_frame, key_frame)


def merge_kernel(last, a_ref, a_log_ref, b_ref, b_log_ref, *outs):
    a_log = a_log_ref[...]
    b_log, b_power = unpack_stats(b_log_ref[...])
    top = jnp.maximum(a_log, b_log)
    a_weight, b_weight = jnp.exp2(a_log - top), jnp.exp2(b_log - top)
    total = a_weight + b_weight
    a_share, b_share = a_weight / total, b_weight / total * (jnp.exp2(b_power) * (1.0 / STEPS))
    rows = a_log.shape[0]
    half = rows if last else rows // 2
    lane = lax.broadcasted_iota(jnp.int32, (half, LANES), 1)
    powers = jnp.zeros((half, LANES), jnp.float32)
    for head in range(HEADS):
        cols = slice(head * HEAD_DIM, (head + 1) * HEAD_DIM)
        o = a_ref[:, cols] * a_share[:, head : head + 1] + unpack(b_ref[:, cols]) * b_share[:, head : head + 1]
        outs[0][:, cols] = o[:half].astype(outs[0].dtype)
        if not last:
            outs[2][:, cols], power = pack(o[half:])
            powers = jnp.where(lane == head, power, powers)
    if not last:
        log_sum = jnp.maximum(top + jnp.log2(total), LOG_FLOOR)
        outs[1][...] = log_sum[:half]
        outs[3][...] = pack_stats(log_sum[half:], powers)


def merge(a, a_log, b, b_log, last):
    rows = a.shape[0]
    half = rows // 2
    if last:
        shapes = [jax.ShapeDtypeStruct((rows, WIDTH), jnp.bfloat16)]
    else:
        shapes = [
            jax.ShapeDtypeStruct((half, WIDTH), jnp.float32),
            jax.ShapeDtypeStruct((half, LANES), jnp.float32),
            jax.ShapeDtypeStruct((half, WIDTH), jnp.int16),
            jax.ShapeDtypeStruct((half, LANES), jnp.int16),
        ]
    vmem = pl.BlockSpec(memory_space=pltpu.VMEM)
    return pl.pallas_call(
        functools.partial(merge_kernel, last),
        in_specs=[vmem] * 4,
        out_specs=[vmem] * len(shapes),
        out_shape=shapes,
        compiler_params=pltpu.CompilerParams(vmem_limit_bytes=16 << 20),
        name="merge",
    )(a, a_log, b, b_log)


def strides(devices):
    order = []
    stride = 2
    while stride < devices:
        order.append(stride)
        stride *= 2
    if len(order) >= 2:
        order = order[1:] + order[:1]
    return order + [1]


def local(devices, queries, cache_keys, cache_values, span_keys, span_values, cache_tokens, span_start):
    me = lax.axis_index("seq")
    cache_rows, own = cache_keys.shape[0], queries.shape[0]
    order = strides(devices)

    def swap(x, stride):
        return lax.ppermute(x, "seq", [(i, i ^ stride) for i in range(devices)])

    q, holder = queries, [0]
    for stride in order:
        q = jnp.concatenate([q, swap(q, stride)], axis=0)
        holder = holder + [h ^ stride for h in holder]
    position = (me ^ jnp.array(holder, jnp.int32))[:, None] * own + jnp.arange(own, dtype=jnp.int32)[None, :]
    query_frame = (span_start[0] + position.reshape(-1)) // FRAME_TOK
    query_frame = jnp.broadcast_to(query_frame[:, None], (devices * own, LANES))
    key_frame = (span_start[0] + me * own + jnp.arange(own, dtype=jnp.int32)) // FRAME_TOK
    key_frame = jnp.broadcast_to(key_frame[None, :], (8, own))
    limit = jnp.clip(cache_tokens - me * cache_rows, 0, cache_rows)
    keep, keep_log, send, send_log = attend(
        limit, q, cache_keys, cache_values, span_keys, span_values, query_frame, key_frame
    )
    for stride in order[:0:-1]:
        got, got_log = swap(send, stride), swap(send_log, stride)
        keep, keep_log, send, send_log = merge(keep, keep_log, got, got_log, False)
    got, got_log = swap(send, order[0]), swap(send_log, order[0])
    return merge(keep, keep_log, got, got_log, True)[0]


def solution(mesh):
    rows = P(("groups", "seq"), None)
    placed = (rows, rows, rows, rows, rows, P("groups"), P("groups"))
    return jax.shard_map(
        functools.partial(local, mesh.shape["seq"]), mesh=mesh, in_specs=placed, out_specs=rows, check_vma=False
    )
```

time: 237 us -> 69.1 us (0.29)
  blocking collectives: 141 us -> 0 us
  local copies, waits for them, and re-layouts: 49 us -> 7.64 us
  waiting for transfers between devices: 0.02 us -> 21.2 us
  matrix products: 21 us -> 0 us
  Pallas kernels: 0 us -> 20 us
  starting transfers between devices: 0.01 us -> 15 us
  between operations: 15.5 us -> 1.41 us
  other arithmetic: 8.89 us -> 3.24 us
    unnamed x1 -> x0, blocking collectives: 57.8 us -> none
    pmax x1 -> x0, blocking collectives: 57.8 us -> none  [local(): row_top = lax.pmax(local_top, 'seq')]
    all_gather x1 -> x0, blocking collectives: 25.4 us -> none  [local(): all_queries = lax.all_gather(queries, 'seq', axis=0, tiled=True)]
    dynamic_slice x4 -> x0, local copies, waits for them, and re-layouts: 22.4 us -> none  [sum_step(): scores = lax.dynamic_index_in_dim(stored, step_index, 0, keepdims=False)]
    ppermute x0 -> x12, waiting for transfers between devices: none -> 21.2 us  [swap(): return lax.ppermute(x, 'seq', [(i, i ^ stride) for i in range(devices)])]
    dot_general x6 -> x0, matrix products: 21 us -> none  [the longest x2 10.9 us: block_scores(): jnp.einsum('qhd,khd->hqk', query_heads, key_piece, preferred_element_type...]
    pallas_call x0 -> x5, Pallas kernels: none -> 20 us  [the longest x1 14.7 us: attend(): pl.pallas_call(attend_kernel, grid_spec=pltpu.PrefetchScalarGridSpec(num_...]
    ppermute x0 -> x12, starting transfers between devices: none -> 15 us  [swap(): return lax.ppermute(x, 'seq', [(i, i ^ stride) for i in range(devices)])]
  transfers between devices with their start and end apart: 1 -> 12, of which waited for: 0 -> 7; matrix products, arithmetic and copies ran while one was open for 0% -> 3% of each run, Pallas kernels for 0% -> 0%
where the time goes in v1:
time: 69.1 us; the launch traced here: 68.5 us
  waiting for transfers between devices  21.2 us (31%)
  Pallas kernels  20 us (29%)
  starting transfers between devices  15 us (22%)
  local copies, waits for them, and re-layouts  7.64 us (11%)
  other arithmetic  3.24 us (5%)
  between operations  1.41 us (2%)
    ppermute x12, waiting for transfers between devices, swap(): return lax.ppermute(x, 'seq', [(i, i ^ stride) for i in range(devices)])  21.2 us
    ppermute x12, starting transfers between devices, swap(): return lax.ppermute(x, 'seq', [(i, i ^ stride) for i in range(devices)])  15 us
    pallas_call x1, Pallas kernels, attend(): pl.pallas_call(attend_kernel, grid_spec=pltpu.PrefetchScalarGridSpec(num_...  14.7 us
    unnamed x12, local copies, waits for them, and re-layouts  7.36 us
    pallas_call x4, Pallas kernels, merge(): pl.pallas_call(functools.partial(merge_kernel, last), in_specs=[vmem] * 4...  5.29 us
    concatenate x3, other arithmetic, local(): q = jnp.concatenate([q, swap(q, stride)], axis=0)  2.38 us
  transfers between devices with their start and end apart: 12, of which 7 were waited for; matrix products, arithmetic and copies ran while one was open for 3% of the time, Pallas kernels for 0%

profile of v1, /device:TPU:0, one launch (start us, length us, event | category | flops | bytes accessed | tf_op | source)
XLA Modules:
  0.0 68.5 jit_solution(16442129260628659154)
XLA Ops:
  0.0 3.1 %collective-permute-start = (bf16[8,2560]{1,0:T(8,128)(2,1)}, bf16[8,2560]{1,0:T(8,128)(2,1)S(1)}, u32[]{:S(2)}, u32[]{:S(2)}) collective-permute-start(bf16[8,2560]{1,0:T(8,128)(2,1)} %param.8), channel_id=1, source_target_pairs={{0,4},{1,5},{2,6},{3,7},{4,0},{5,1},{6,2},{7,3},{8,12},{9,13},{10,... | collective-permute-start | bytes 122888 | tf_op jit(solution)/shard_map/ppermute | solution.py:190
  3.1 0.8 %constant_dynamic-update-slice_fusion.4 = bf16[128,2560]{1,0:T(8,128)(2,1)S(1)} fusion(bf16[8,2560]{1,0:T(8,128)(2,1)} %param.8), kind=kLoop, calls=%fused_computation.7 | loop fusion | bytes 81920
  4.5 0.7 xor_multiply_fusion
  5.2 0.1 fusion
  5.3 0.1 div.24
  5.4 0.1 fusion.1
  5.5 0.1 reshape.47
  6.2 0.0 collective-permute-done
  6.2 0.8 %pad_maximum_fusion.2 = bf16[16,2560]{1,0:T(8,128)(2,1)S(1)} fusion(bf16[8,2560]{1,0:T(8,128)(2,1)S(1)} %collective-permute-done, bf16[8,2560]{1,0:T(8,128)(2,1)} %param.8), kind=kLoop, calls=%fused_computation.2 | loop fusion | flops 163840 | bytes 163840 | tf_op jit(solution)/shard_map/concatenate | solution.py:194
  7.0 2.6 %collective-permute-start.1 = (bf16[16,2560]{1,0:T(8,128)(2,1)S(1)}, bf16[16,2560]{1,0:T(8,128)(2,1)S(1)}, u32[]{:S(2)}, u32[]{:S(2)}) collective-permute-start(bf16[16,2560]{1,0:T(8,128)(2,1)S(1)} %pad_maximum_fusion.2), channel_id=1, source_target_pairs={{0,8},{1,9},{2,10},{3,11},{4,12},{5,13},{6,14},{7,15},{8,0},{9,1},... | collective-permute-start | bytes 245768 | tf_op jit(solution)/shard_map/ppermute | solution.py:190
  9.6 3.8 %collective-permute-done.1 = bf16[16,2560]{1,0:T(8,128)(2,1)S(1)} collective-permute-done((bf16[16,2560]{1,0:T(8,128)(2,1)S(1)}, bf16[16,2560]{1,0:T(8,128)(2,1)S(1)}, u32[]{:S(2)}, u32[]{:S(2)}) %collective-permute-start.1) | collective-permute-done | bytes 81952 | tf_op jit(solution)/shard_map/ppermute | solution.py:190
  13.4 0.8 %pad_maximum_fusion.1 = bf16[32,2560]{1,0:T(8,128)(2,1)S(1)} fusion(bf16[16,2560]{1,0:T(8,128)(2,1)S(1)} %collective-permute-done.1, bf16[8,2560]{1,0:T(8,128)(2,1)S(1)} %collective-permute-done, bf16[8,2560]{1,0:T(8,128)(2,1)} %param.8), kind=kLoop, calls=%fused_computation.1 | loop fusion | flops 491520 | bytes 327680 | tf_op jit(solution)/shard_map/concatenate | solution.py:194
  14.2 1.6 %collective-permute-start.2 = (bf16[32,2560]{1,0:T(8,128)(2,1)S(1)}, bf16[32,2560]{1,0:T(8,128)(2,1)S(1)}, u32[]{:S(2)}, u32[]{:S(2)}) collective-permute-start(bf16[32,2560]{1,0:T(8,128)(2,1)S(1)} %pad_maximum_fusion.1), channel_id=1, source_target_pairs={{0,2},{1,3},{2,0},{3,1},{4,6},{5,7},{6,4},{7,5},{8,10},{9,11},{10,... | collective-permute-start | bytes 491528 | tf_op jit(solution)/shard_map/ppermute | solution.py:190
  15.9 3.7 %collective-permute-done.2 = bf16[32,2560]{1,0:T(8,128)(2,1)S(1)} collective-permute-done((bf16[32,2560]{1,0:T(8,128)(2,1)S(1)}, bf16[32,2560]{1,0:T(8,128)(2,1)S(1)}, u32[]{:S(2)}, u32[]{:S(2)}) %collective-permute-start.2) | collective-permute-done | bytes 163872 | tf_op jit(solution)/shard_map/ppermute | solution.py:190
  19.6 0.8 %pad_maximum_fusion = bf16[64,2560]{1,0:T(8,128)(2,1)S(1)} fusion(bf16[32,2560]{1,0:T(8,128)(2,1)S(1)} %collective-permute-done.2, bf16[16,2560]{1,0:T(8,128)(2,1)S(1)} %collective-permute-done.1, bf16[8,2560]{1,0:T(8,128)(2,1)S(1)} %collective-permute-done, bf16[8,2560]{1,0:T(8,128)(2,1)} %param.8), kind=kLoop, calls=%fused_computation | loop fusion | flops 1310720 | bytes 655360 | tf_op jit(solution)/shard_map/concatenate | solution.py:194
  20.4 0.1 collective-permute-start.3
  20.5 1.6 %collective-permute-done.3 = bf16[64,2560]{1,0:T(8,128)(2,1)S(1)} collective-permute-done((bf16[64,2560]{1,0:T(8,128)(2,1)S(1)}, bf16[64,2560]{1,0:T(8,128)(2,1)S(1)}, u32[]{:S(2)}, u32[]{:S(2)}) %collective-permute-start.3) | collective-permute-done | bytes 327712 | tf_op jit(solution)/shard_map/ppermute | solution.py:190
  22.1 0.1 broadcast_in_dim.4.qf_ref
  22.2 0.0 copy-start
  22.2 2.5 %copy-done = bf16[1024,2560]{1,0:T(8,128)(2,1)S(1)} copy-done((bf16[1024,2560]{1,0:T(8,128)(2,1)S(1)}, bf16[1024,2560]{1,0:T(8,128)(2,1)}, u32[]{:S(2)}) %copy-start) | copy-done | bytes 5242904
  24.7 0.0 copy-start.1
  24.7 2.5 %copy-done.1 = bf16[1024,2560]{1,0:T(8,128)(2,1)S(1)} copy-done((bf16[1024,2560]{1,0:T(8,128)(2,1)S(1)}, bf16[1024,2560]{1,0:T(8,128)(2,1)}, u32[]{:S(2)}) %copy-start.1) | copy-done | bytes 5242904
  27.2 0.0 copy-start.2
  27.2 0.8 %copy-done.2 = bf16[8,2560]{1,0:T(8,128)(2,1)S(1)} copy-done((bf16[8,2560]{1,0:T(8,128)(2,1)S(1)}, bf16[8,2560]{1,0:T(8,128)(2,1)}, u32[]{:S(2)}) %copy-start.2) | copy-done | bytes 40984
  28.0 0.0 copy-start.3
  28.0 0.8 %copy-done.3 = bf16[8,2560]{1,0:T(8,128)(2,1)S(1)} copy-done((bf16[8,2560]{1,0:T(8,128)(2,1)S(1)}, bf16[8,2560]{1,0:T(8,128)(2,1)}, u32[]{:S(2)}) %copy-start.3) | copy-done | bytes 40984
  28.8 14.7 %attend.1 = (f32[64,2560]{1,0:T(8,128)S(1)}, f32[64,128]{1,0:T(8,128)S(1)}, s16[64,2560]{1,0:T(8,128)(2,1)S(1)}, s16[64,128]{1,0:T(8,128)(2,1)S(1)}) custom-call(s32[1]{0:T(128)S(6)} %min.6.limit_ref, bf16[128,2560]{1,0:T(8,128)(2,1)S(1)} %constant_dynamic-update-slice_fusion.q_ref, bf16[1024,2560]{1,0:T(8,128)(2,1)S(1)} %copy-done, ...), custom_call_target="tpu_custom_call" | custom-call | tf_op jit(solution)/shard_map/attend/pallas_call | solution.py:106
  43.5 0.2 collective-permute-start.4
  43.7 0.4 collective-permute-start.5
  44.0 1.1 %collective-permute-done.5.b_log_ref = s16[64,128]{1,0:T(8,128)(2,1)S(1)} collective-permute-done((s16[64,128]{1,0:T(8,128)(2,1)S(1)}, s16[64,128]{1,0:T(8,128)(2,1)S(1)}, u32[]{:S(2)}, u32[]{:S(2)}) %collective-permute-start.5) | collective-permute-done | bytes 16416 | tf_op jit(solution)/shard_map/ppermute | solution.py:190
  45.2 0.0 collective-permute-done.4.b_ref
  45.2 2.0 %merge.4 = (f32[32,2560]{1,0:T(8,128)S(1)}, f32[32,128]{1,0:T(8,128)S(1)}, s16[32,2560]{1,0:T(8,128)(2,1)S(1)}, s16[32,128]{1,0:T(8,128)(2,1)S(1)}) custom-call(f32[64,2560]{1,0:T(8,128)S(1)} %get-tuple-element.21.a_ref, f32[64,128]{1,0:T(8,128)S(1)} %get-tuple-element.22.a_log_ref, s16[64,2560]{1,0:T(8,128)(2,1)S(1)} %collective-permute-done.4.b_ref, ...), custom_call_target="tpu_custom_call" | custom-call | tf_op jit(solution)/shard_map/merge/pallas_call | solution.py:163
  47.2 1.6 %collective-permute-start.6 = (s16[32,2560]{1,0:T(8,128)(2,1)S(1)}, s16[32,2560]{1,0:T(8,128)(2,1)S(1)}, u32[]{:S(2)}, u32[]{:S(2)}) collective-permute-start(s16[32,2560]{1,0:T(8,128)(2,1)S(1)} %get-tuple-element.27), channel_id=1, source_target_pairs={{0,2},{1,3},{2,0},{3,1},{4,6},{5,7},{6,4},{7,5},{8,10},{9,11},{10,... | collective-permute-start | bytes 491528 | tf_op jit(solution)/shard_map/ppermute | solution.py:190
  48.8 0.5 collective-permute-start.7
  49.2 4.4 %collective-permute-done.7.b_log_ref = s16[32,128]{1,0:T(8,128)(2,1)S(1)} collective-permute-done((s16[32,128]{1,0:T(8,128)(2,1)S(1)}, s16[32,128]{1,0:T(8,128)(2,1)S(1)}, u32[]{:S(2)}, u32[]{:S(2)}) %collective-permute-start.7) | collective-permute-done | bytes 8224 | tf_op jit(solution)/shard_map/ppermute | solution.py:190
  53.6 0.0 collective-permute-done.6.b_ref
  53.6 1.6 %merge.5 = (f32[16,2560]{1,0:T(8,128)S(1)}, f32[16,128]{1,0:T(8,128)S(1)}, s16[16,2560]{1,0:T(8,128)(2,1)S(1)}, s16[16,128]{1,0:T(8,128)(2,1)S(1)}) custom-call(f32[32,2560]{1,0:T(8,128)S(1)} %get-tuple-element.25.a_ref, f32[32,128]{1,0:T(8,128)S(1)} %get-tuple-element.26.a_log_ref, s16[32,2560]{1,0:T(8,128)(2,1)S(1)} %collective-permute-done.6.b_ref, ...), custom_call_target="tpu_custom_call" | custom-call | tf_op jit(solution)/shard_map/merge/pallas_call | solution.py:163
  55.3 1.7 %collective-permute-start.8 = (s16[16,2560]{1,0:T(8,128)(2,1)S(1)}, s16[16,2560]{1,0:T(8,128)(2,1)S(1)}, u32[]{:S(2)}, u32[]{:S(2)}) collective-permute-start(s16[16,2560]{1,0:T(8,128)(2,1)S(1)} %get-tuple-element.31), channel_id=1, source_target_pairs={{0,8},{1,9},{2,10},{3,11},{4,12},{5,13},{6,14},{7,15},{8,0},{9,1},... | collective-permute-start | bytes 245768 | tf_op jit(solution)/shard_map/ppermute | solution.py:190
  56.9 1.3 %collective-permute-start.9 = (s16[16,128]{1,0:T(8,128)(2,1)S(1)}, s16[16,128]{1,0:T(8,128)(2,1)S(1)}, u32[]{:S(2)}, u32[]{:S(2)}) collective-permute-start(s16[16,128]{1,0:T(8,128)(2,1)S(1)} %get-tuple-element.32), channel_id=1, source_target_pairs={{0,8},{1,9},{2,10},{3,11},{4,12},{5,13},{6,14},{7,15},{8,0},{9,1},... | collective-permute-start | bytes 12296 | tf_op jit(solution)/shard_map/ppermute | solution.py:190
  58.2 3.5 %collective-permute-done.9.b_log_ref = s16[16,128]{1,0:T(8,128)(2,1)S(1)} collective-permute-done((s16[16,128]{1,0:T(8,128)(2,1)S(1)}, s16[16,128]{1,0:T(8,128)(2,1)S(1)}, u32[]{:S(2)}, u32[]{:S(2)}) %collective-permute-start.9) | collective-permute-done | bytes 4128 | tf_op jit(solution)/shard_map/ppermute | solution.py:190
  61.7 0.0 collective-permute-done.8.b_ref
  61.7 0.8 %merge.6 = (f32[8,2560]{1,0:T(8,128)S(1)}, f32[8,128]{1,0:T(8,128)S(1)}, s16[8,2560]{1,0:T(8,128)(2,1)S(1)}, s16[8,128]{1,0:T(8,128)(2,1)S(1)}) custom-call(f32[16,2560]{1,0:T(8,128)S(1)} %get-tuple-element.29.a_ref, f32[16,128]{1,0:T(8,128)S(1)} %get-tuple-element.30.a_log_ref, s16[16,2560]{1,0:T(8,128)(2,1)S(1)} %collective-permute-done.8.b_ref, ...), custom_call_target="tpu_custom_call" | custom-call | tf_op jit(solution)/shard_map/merge/pallas_call | solution.py:163
  62.5 1.5 %collective-permute-start.10 = (s16[8,2560]{1,0:T(8,128)(2,1)S(1)}, s16[8,2560]{1,0:T(8,128)(2,1)S(1)}, u32[]{:S(2)}, u32[]{:S(2)}) collective-permute-start(s16[8,2560]{1,0:T(8,128)(2,1)S(1)} %get-tuple-element.35), channel_id=1, source_target_pairs={{0,4},{1,5},{2,6},{3,7},{4,0},{5,1},{6,2},{7,3},{8,12},{9,13},{10,... | collective-permute-start | bytes 122888 | tf_op jit(solution)/shard_map/ppermute | solution.py:190
  64.0 0.5 collective-permute-start.11
  64.6 3.1 %collective-permute-done.11.b_log_ref = s16[8,128]{1,0:T(8,128)(2,1)S(1)} collective-permute-done((s16[8,128]{1,0:T(8,128)(2,1)S(1)}, s16[8,128]{1,0:T(8,128)(2,1)S(1)}, u32[]{:S(2)}, u32[]{:S(2)}) %collective-permute-start.11) | collective-permute-done | bytes 2080 | tf_op jit(solution)/shard_map/ppermute | solution.py:190
  67.6 0.0 collective-permute-done.10.b_ref
  67.6 0.8 %merge.7 = bf16[8,2560]{1,0:T(8,128)(2,1)} custom-call(f32[8,2560]{1,0:T(8,128)S(1)} %get-tuple-element.33.a_ref, f32[8,128]{1,0:T(8,128)S(1)} %get-tuple-element.34.a_log_ref, s16[8,2560]{1,0:T(8,128)(2,1)S(1)} %collective-permute-done.10.b_ref, s16[8,128]{1,0:T(8,128)(2,1)S(1)} %collective-permute-done.11.b_log_ref), custom_call_target="tpu_custom_call" | custom-call | tf_op jit(solution)/shard_map/merge/pallas_call | solution.py:163
  (7 shorter events, 0.1 us)
Async XLA Ops:
  0.0 6.2 %collective-permute-start = (bf16[8,2560]{1,0:T(8,128)(2,1)}, bf16[8,2560]{1,0:T(8,128)(2,1)S(1)}, u32[]{:S(2)}, u32[]{:S(2)}) collective-permute-start(bf16[8,2560]{1,0:T(8,128)(2,1)} %param.8), channel_id=1, source_target_pairs={{0,4},{1,5},{2,6},{3,7},{4,0},{5,1},{6,2},{7,3},{8,12},{9,13},{10,... | collective-permute-start | bytes 122888 | tf_op jit(solution)/shard_map/ppermute | solution.py:190
  7.0 6.4 %collective-permute-start.1 = (bf16[16,2560]{1,0:T(8,128)(2,1)S(1)}, bf16[16,2560]{1,0:T(8,128)(2,1)S(1)}, u32[]{:S(2)}, u32[]{:S(2)}) collective-permute-start(bf16[16,2560]{1,0:T(8,128)(2,1)S(1)} %pad_maximum_fusion.2), channel_id=1, source_target_pairs={{0,8},{1,9},{2,10},{3,11},{4,12},{5,13},{6,14},{7,15},{8,0},{9,1},... | collective-permute-start | bytes 245768 | tf_op jit(solution)/shard_map/ppermute | solution.py:190
  14.2 5.4 %collective-permute-start.2 = (bf16[32,2560]{1,0:T(8,128)(2,1)S(1)}, bf16[32,2560]{1,0:T(8,128)(2,1)S(1)}, u32[]{:S(2)}, u32[]{:S(2)}) collective-permute-start(bf16[32,2560]{1,0:T(8,128)(2,1)S(1)} %pad_maximum_fusion.1), channel_id=1, source_target_pairs={{0,2},{1,3},{2,0},{3,1},{4,6},{5,7},{6,4},{7,5},{8,10},{9,11},{10,... | collective-permute-start | bytes 491528 | tf_op jit(solution)/shard_map/ppermute | solution.py:190
  20.4 1.7 %collective-permute-start.3 = (bf16[64,2560]{1,0:T(8,128)(2,1)S(1)}, bf16[64,2560]{1,0:T(8,128)(2,1)S(1)}, u32[]{:S(2)}, u32[]{:S(2)}) collective-permute-start(bf16[64,2560]{1,0:T(8,128)(2,1)S(1)} %pad_maximum_fusion), channel_id=1, source_target_pairs={{0,1},{1,0},{2,3},{3,2},{4,5},{5,4},{6,7},{7,6},{8,9},{9,8},{10,11... | collective-permute-start | bytes 983048 | tf_op jit(solution)/shard_map/ppermute | solution.py:190
  22.2 2.5 %copy-start = (bf16[1024,2560]{1,0:T(8,128)(2,1)S(1)}, bf16[1024,2560]{1,0:T(8,128)(2,1)}, u32[]{:S(2)}) copy-start(bf16[1024,2560]{1,0:T(8,128)(2,1)} %k_ref.1) | copy-start | bytes 15728644
  24.7 2.5 %copy-start.1 = (bf16[1024,2560]{1,0:T(8,128)(2,1)S(1)}, bf16[1024,2560]{1,0:T(8,128)(2,1)}, u32[]{:S(2)}) copy-start(bf16[1024,2560]{1,0:T(8,128)(2,1)} %v_ref.1) | copy-start | bytes 15728644
  27.2 0.8 %copy-start.2 = (bf16[8,2560]{1,0:T(8,128)(2,1)S(1)}, bf16[8,2560]{1,0:T(8,128)(2,1)}, u32[]{:S(2)}) copy-start(bf16[8,2560]{1,0:T(8,128)(2,1)} %sk_ref.1) | copy-start | bytes 122884
  28.0 0.8 %copy-start.3 = (bf16[8,2560]{1,0:T(8,128)(2,1)S(1)}, bf16[8,2560]{1,0:T(8,128)(2,1)}, u32[]{:S(2)}) copy-start(bf16[8,2560]{1,0:T(8,128)(2,1)} %sv_ref.1) | copy-start | bytes 122884
  43.5 1.7 %collective-permute-start.4 = (s16[64,2560]{1,0:T(8,128)(2,1)S(1)}, s16[64,2560]{1,0:T(8,128)(2,1)S(1)}, u32[]{:S(2)}, u32[]{:S(2)}) collective-permute-start(s16[64,2560]{1,0:T(8,128)(2,1)S(1)} %get-tuple-element.23), channel_id=1, source_target_pairs={{0,1},{1,0},{2,3},{3,2},{4,5},{5,4},{6,7},{7,6},{8,9},{9,8},{10,11... | collective-permute-start | bytes 983048 | tf_op jit(solution)/shard_map/ppermute | solution.py:190
  43.7 1.5 %collective-permute-start.5 = (s16[64,128]{1,0:T(8,128)(2,1)S(1)}, s16[64,128]{1,0:T(8,128)(2,1)S(1)}, u32[]{:S(2)}, u32[]{:S(2)}) collective-permute-start(s16[64,128]{1,0:T(8,128)(2,1)S(1)} %get-tuple-element.24), channel_id=1, source_target_pairs={{0,1},{1,0},{2,3},{3,2},{4,5},{5,4},{6,7},{7,6},{8,9},{9,8},{10,11... | collective-permute-start | bytes 49160 | tf_op jit(solution)/shard_map/ppermute | solution.py:190
  47.2 6.5 %collective-permute-start.6 = (s16[32,2560]{1,0:T(8,128)(2,1)S(1)}, s16[32,2560]{1,0:T(8,128)(2,1)S(1)}, u32[]{:S(2)}, u32[]{:S(2)}) collective-permute-start(s16[32,2560]{1,0:T(8,128)(2,1)S(1)} %get-tuple-element.27), channel_id=1, source_target_pairs={{0,2},{1,3},{2,0},{3,1},{4,6},{5,7},{6,4},{7,5},{8,10},{9,11},{10,... | collective-permute-start | bytes 491528 | tf_op jit(solution)/shard_map/ppermute | solution.py:190
  48.8 4.8 %collective-permute-start.7 = (s16[32,128]{1,0:T(8,128)(2,1)S(1)}, s16[32,128]{1,0:T(8,128)(2,1)S(1)}, u32[]{:S(2)}, u32[]{:S(2)}) collective-permute-start(s16[32,128]{1,0:T(8,128)(2,1)S(1)} %get-tuple-element.28), channel_id=1, source_target_pairs={{0,2},{1,3},{2,0},{3,1},{4,6},{5,7},{6,4},{7,5},{8,10},{9,11},{10,... | collective-permute-start | bytes 24584 | tf_op jit(solution)/shard_map/ppermute | solution.py:190
  55.3 6.4 %collective-permute-start.8 = (s16[16,2560]{1,0:T(8,128)(2,1)S(1)}, s16[16,2560]{1,0:T(8,128)(2,1)S(1)}, u32[]{:S(2)}, u32[]{:S(2)}) collective-permute-start(s16[16,2560]{1,0:T(8,128)(2,1)S(1)} %get-tuple-element.31), channel_id=1, source_target_pairs={{0,8},{1,9},{2,10},{3,11},{4,12},{5,13},{6,14},{7,15},{8,0},{9,1},... | collective-permute-start | bytes 245768 | tf_op jit(solution)/shard_map/ppermute | solution.py:190
  56.9 4.8 %collective-permute-start.9 = (s16[16,128]{1,0:T(8,128)(2,1)S(1)}, s16[16,128]{1,0:T(8,128)(2,1)S(1)}, u32[]{:S(2)}, u32[]{:S(2)}) collective-permute-start(s16[16,128]{1,0:T(8,128)(2,1)S(1)} %get-tuple-element.32), channel_id=1, source_target_pairs={{0,8},{1,9},{2,10},{3,11},{4,12},{5,13},{6,14},{7,15},{8,0},{9,1},... | collective-permute-start | bytes 12296 | tf_op jit(solution)/shard_map/ppermute | solution.py:190
  62.5 5.1 %collective-permute-start.10 = (s16[8,2560]{1,0:T(8,128)(2,1)S(1)}, s16[8,2560]{1,0:T(8,128)(2,1)S(1)}, u32[]{:S(2)}, u32[]{:S(2)}) collective-permute-start(s16[8,2560]{1,0:T(8,128)(2,1)S(1)} %get-tuple-element.35), channel_id=1, source_target_pairs={{0,4},{1,5},{2,6},{3,7},{4,0},{5,1},{6,2},{7,3},{8,12},{9,13},{10,... | collective-permute-start | bytes 122888 | tf_op jit(solution)/shard_map/ppermute | solution.py:190
  64.0 3.6 %collective-permute-start.11 = (s16[8,128]{1,0:T(8,128)(2,1)S(1)}, s16[8,128]{1,0:T(8,128)(2,1)S(1)}, u32[]{:S(2)}, u32[]{:S(2)}) collective-permute-start(s16[8,128]{1,0:T(8,128)(2,1)S(1)} %get-tuple-element.36), channel_id=1, source_target_pairs={{0,4},{1,5},{2,6},{3,7},{4,0},{5,1},{6,2},{7,3},{8,12},{9,13},{10,... | collective-permute-start | bytes 6152 | tf_op jit(solution)/shard_map/ppermute | solution.py:190

commit v2 on v1

v2 whole, which is shorter than its diff:
```python
import functools
import math

import jax
import jax.numpy as jnp
from jax import lax
from jax.experimental import pallas as pl
from jax.experimental.pallas import tpu as pltpu
from jax.sharding import PartitionSpec as P

HEAD_DIM = 128
HEADS = 20
FRAME_TOK = 1560
LANES = 128
PART = 32
NEG_FILL = -1e30
LOG_FLOOR = -30000.0
FIXED = 32768.0
HALF_RANGE = 32768
STEPS = 32512.0
PEAK_FLOOR = 1e-30
SCALE = math.log2(math.e) / math.sqrt(HEAD_DIM)
WIDTH = HEADS * HEAD_DIM


def pack(o):
    peak = jnp.max(jnp.abs(o), axis=1, keepdims=True)
    power = jnp.ceil(jnp.log2(jnp.maximum(peak, PEAK_FLOOR)))
    steps = jnp.round(o * (jnp.exp2(-power) * STEPS))
    return steps.astype(jnp.int32).astype(jnp.int16), power


def unpack(steps):
    return steps.astype(jnp.int32).astype(jnp.float32)


def pack_stats(log_sum, power):
    fixed = jnp.round(log_sum * FIXED).astype(jnp.int32)
    high = fixed // HALF_RANGE
    low = fixed - high * HALF_RANGE
    lane = lax.broadcasted_iota(jnp.int32, log_sum.shape, 1)
    packed = jnp.where(lane < PART, high, pltpu.roll(low, PART, 1))
    packed = jnp.where(lane < 2 * PART, packed, pltpu.roll(power.astype(jnp.int32), 2 * PART, 1))
    return packed.astype(jnp.int16)


def unpack_stats(packed):
    packed = packed.astype(jnp.int32)
    fixed = packed * HALF_RANGE + pltpu.roll(packed, LANES - PART, 1)
    power = pltpu.roll(packed, LANES - 2 * PART, 1)
    return fixed.astype(jnp.float32) * (1.0 / FIXED), power.astype(jnp.float32)


def attend_kernel(
    limit_ref, q_ref, k_hbm, v_hbm, sk_ref, sv_ref, qf_ref, kf_ref, keep_ref, keep_log_ref, send_ref, k_ref, v_ref, sems
):
    copies = []
    for head in range(HEADS):
        cols = pl.ds(head * HEAD_DIM, HEAD_DIM)
        pair = [
            pltpu.make_async_copy(k_hbm.at[:, cols], k_ref.at[:, cols], sems.at[head, 0]),
            pltpu.make_async_copy(v_hbm.at[:, cols], v_ref.at[:, cols], sems.at[head, 1]),
        ]
        for copy in pair:
            copy.start()
        copies.append(pair)
    rows, keys = q_ref.shape[0], k_ref.shape[0]
    half = rows // 2
    bias = jnp.where(lax.broadcasted_iota(jnp.int32, (1, keys), 1) < limit_ref[0], 0.0, NEG_FILL)
    span_bias = jnp.where(kf_ref[0:1, :] <= qf_ref[:, 0:1], 0.0, NEG_FILL)
    lane = lax.broadcasted_iota(jnp.int32, (rows, LANES), 1)
    logs = jnp.zeros((rows, LANES), jnp.float32)
    powers = jnp.zeros((rows - half, LANES), jnp.float32)
    contract_last = (((1,), (1,)), ((), ()))
    dot = functools.partial(jnp.dot, preferred_element_type=jnp.float32)
    for head in range(HEADS):
        cols = slice(head * HEAD_DIM, (head + 1) * HEAD_DIM)
        q = q_ref[:, cols]
        copies[head][0].wait()
        s = lax.dot_general(q, k_ref[:, cols], contract_last, preferred_element_type=jnp.float32) + bias
        s2 = lax.dot_general(q, sk_ref[:, cols], contract_last, preferred_element_type=jnp.float32) + span_bias
        top = jnp.maximum(jnp.max(s, axis=1, keepdims=True), jnp.max(s2, axis=1, keepdims=True))
        p = jnp.exp2((s - top) * SCALE)
        p2 = jnp.exp2((s2 - top) * SCALE)
        total = jnp.sum(p, axis=1, keepdims=True) + jnp.sum(p2, axis=1, keepdims=True)
        high, high2 = p.astype(jnp.bfloat16), p2.astype(jnp.bfloat16)
        low = (p - high.astype(jnp.float32)).astype(jnp.bfloat16)
        low2 = (p2 - high2.astype(jnp.float32)).astype(jnp.bfloat16)
        copies[head][1].wait()
        v, sv = v_ref[:, cols], sv_ref[:, cols]
        o = (dot(high, v) + dot(low, v) + dot(high2, sv) + dot(low2, sv)) * (1.0 / total)
        log_sum = jnp.maximum(top * SCALE + jnp.log2(total), LOG_FLOOR)
        keep_ref[:, cols] = o[:half]
        send_ref[:, cols], power = pack(o[half:])
        logs = jnp.where(lane == head, log_sum, logs)
        powers = jnp.where(lane[half:] == head, power, powers)
    keep_log_ref[...] = logs[:half]
    send_ref[:, WIDTH:] = pack_stats(logs[half:], powers)


def halves(rows):
    return [
        jax.ShapeDtypeStruct((rows, WIDTH), jnp.float32),
        jax.ShapeDtypeStruct((rows, LANES), jnp.float32),
        jax.ShapeDtypeStruct((rows, WIDTH + LANES), jnp.int16),
    ]


def attend(limit, q, k, v, sk, sv, query_frame, key_frame):
    vmem = pl.BlockSpec(memory_space=pltpu.VMEM)
    hbm = pl.BlockSpec(memory_space=pltpu.HBM)
    rows, keys = q.shape[0], k.shape[0]
    return pl.pallas_call(
        attend_kernel,
        in_specs=[pl.BlockSpec(memory_space=pltpu.SMEM), vmem, hbm, hbm] + [vmem] * 4,
        out_specs=[vmem] * 3,
        out_shape=halves(rows // 2),
        scratch_shapes=[
            pltpu.VMEM(k.shape, k.dtype),
            pltpu.VMEM(v.shape, v.dtype),
            pltpu.SemaphoreType.DMA((HEADS, 2)),
        ],
        compiler_params=pltpu.CompilerParams(vmem_limit_bytes=50 << 20),
        cost_estimate=pl.CostEstimate(
            flops=6 * rows * keys * WIDTH, bytes_accessed=4 * keys * WIDTH, transcendentals=rows * keys * HEADS
        ),
        name="attend",
    )(limit, q, k, v, sk, sv, query_frame, key_frame)


def merge_kernel(last, a_ref, a_log_ref, b_ref, *outs):
    a_log = a_log_ref[...]
    b_log, b_power = unpack_stats(b_ref[:, WIDTH:])
    top = jnp.maximum(a_log, b_log)
    a_weight, b_weight = jnp.exp2(a_log - top), jnp.exp2(b_log - top)
    total = a_weight + b_weight
    a_share, b_share = a_weight / total, b_weight / total * (jnp.exp2(b_power) * (1.0 / STEPS))
    rows = a_log.shape[0]
    half = rows if last else rows // 2
    lane = lax.broadcasted_iota(jnp.int32, (half, LANES), 1)
    powers = jnp.zeros((half, LANES), jnp.float32)
    for head in range(HEADS):
        cols = slice(head * HEAD_DIM, (head + 1) * HEAD_DIM)
        o = a_ref[:, cols] * a_share[:, head : head + 1] + unpack(b_ref[:, cols]) * b_share[:, head : head + 1]
        outs[0][:, cols] = o[:half].astype(outs[0].dtype)
        if not last:
            outs[2][:, cols], power = pack(o[half:])
            powers = jnp.where(lane == head, power, powers)
    if not last:
        log_sum = jnp.maximum(top + jnp.log2(total), LOG_FLOOR)
        outs[1][...] = log_sum[:half]
        outs[2][:, WIDTH:] = pack_stats(log_sum[half:], powers)


def merge(a, a_log, b, last):
    rows = a.shape[0]
    shapes = [jax.ShapeDtypeStruct((rows, WIDTH), jnp.bfloat16)] if last else halves(rows // 2)
    vmem = pl.BlockSpec(memory_space=pltpu.VMEM)
    return pl.pallas_call(
        functools.partial(merge_kernel, last),
        in_specs=[vmem] * 3,
        out_specs=[vmem] * len(shapes),
        out_shape=shapes,
        compiler_params=pltpu.CompilerParams(vmem_limit_bytes=16 << 20),
        name="merge",
    )(a, a_log, b)


def strides(devices):
    order = []
    stride = 2
    while stride < devices:
        order.append(stride)
        stride *= 2
    if len(order) >= 2:
        order = order[1:] + order[:1]
    return order + [1]


def local(devices, queries, cache_keys, cache_values, span_keys, span_values, cache_tokens, span_start):
    me = lax.axis_index("seq")
    cache_rows, own = cache_keys.shape[0], queries.shape[0]
    order = strides(devices)

    def swap(x, stride):
        return lax.ppermute(x, "seq", [(i, i ^ stride) for i in range(devices)])

    q, holder = queries, [0]
    for stride in order:
        q = lax.optimization_barrier(jnp.concatenate([q, swap(q, stride)], axis=0))
        holder = holder + [h ^ stride for h in holder]
    position = (me ^ jnp.array(holder, jnp.int32))[:, None] * own + jnp.arange(own, dtype=jnp.int32)[None, :]
    query_frame = (span_start[0] + position.reshape(-1)) // FRAME_TOK
    query_frame = jnp.broadcast_to(query_frame[:, None], (devices * own, LANES))
    key_frame = (span_start[0] + me * own + jnp.arange(own, dtype=jnp.int32)) // FRAME_TOK
    key_frame = jnp.broadcast_to(key_frame[None, :], (8, own))
    limit = jnp.clip(cache_tokens - me * cache_rows, 0, cache_rows)
    keep, keep_log, send = attend(
        limit, q, cache_keys, cache_values, span_keys, span_values, query_frame, key_frame
    )
    for stride in order[:0:-1]:
        keep, keep_log, send = merge(keep, keep_log, swap(send, stride), False)
    return merge(keep, keep_log, swap(send, order[0]), True)[0]


def solution(mesh):
    rows = P(("groups", "seq"), None)
    placed = (rows, rows, rows, rows, rows, P("groups"), P("groups"))
    return jax.shard_map(
        functools.partial(local, mesh.shape["seq"]), mesh=mesh, in_specs=placed, out_specs=rows, check_vma=False
    )
```

time: 69.1 us -> 64.6 us (0.935)
  local copies, waits for them, and re-layouts: 7.64 us -> 0.27 us
  Pallas kernels: 20 us -> 26.1 us
  other arithmetic: 3.24 us -> 1.71 us
  starting transfers between devices: 15 us -> 13.5 us
    unnamed x12 -> x4, local copies, waits for them, and re-layouts: 7.36 us -> 0.01 us
    pallas_call x5, Pallas kernels: 20 us -> 26.1 us  [the longest x1 20.8 us: attend(): pl.pallas_call(attend_kernel, in_specs=[pl.BlockSpec(memory_space=pltpu.S...]
    concatenate x3 -> x4, other arithmetic: 2.38 us -> 0.86 us  [local(): q = lax.optimization_barrier(jnp.concatenate([q, swap(q, stride)], axis=0))]
    ppermute x12 -> x8, starting transfers between devices: 15 us -> 13.5 us  [swap(): return lax.ppermute(x, 'seq', [(i, i ^ stride) for i in range(devices)])]
    ppermute x12 -> x8, waiting for transfers between devices: 21.2 us -> 21.5 us  [swap(): return lax.ppermute(x, 'seq', [(i, i ^ stride) for i in range(devices)])]
  transfers between devices with their start and end apart: 12 -> 8, of which waited for: 7 -> 8; matrix products, arithmetic and copies ran while one was open for 3% -> 2% of each run, Pallas kernels for 0% -> 0%
where the time goes in v2:
time: 64.6 us; the launch traced here: 64.4 us
  Pallas kernels  26.1 us (40%)
  waiting for transfers between devices  21.5 us (33%)
  starting transfers between devices  13.5 us (21%)
  other arithmetic  1.71 us (3%)
  between operations  1.4 us (2%)
    ppermute x8, waiting for transfers between devices, swap(): return lax.ppermute(x, 'seq', [(i, i ^ stride) for i in range(devices)])  21.5 us
    pallas_call x1, Pallas kernels, attend(): pl.pallas_call(attend_kernel, in_specs=[pl.BlockSpec(memory_space=pltpu.S...  20.8 us
    ppermute x8, starting transfers between devices, swap(): return lax.ppermute(x, 'seq', [(i, i ^ stride) for i in range(devices)])  13.5 us
    pallas_call x4, Pallas kernels, merge(): pl.pallas_call(functools.partial(merge_kernel, last), in_specs=[vmem] * 3...  5.28 us
  transfers between devices with their start and end apart: 8, of which 8 were waited for; matrix products, arithmetic and copies ran while one was open for 2% of the time, Pallas kernels for 0%

profile of v2, /device:TPU:0, one launch (start us, length us, event | category | flops | bytes accessed | tf_op | source)
XLA Modules:
  0.0 64.4 jit_solution(16656295125087358874)
XLA Ops:
  0.0 0.0 copy-start.1
  0.0 0.0 copy-start
  0.0 3.1 %collective-permute-start = (bf16[8,2560]{1,0:T(8,128)(2,1)}, bf16[8,2560]{1,0:T(8,128)(2,1)S(1)}, u32[]{:S(2)}, u32[]{:S(2)}) collective-permute-start(bf16[8,2560]{1,0:T(8,128)(2,1)} %param.8), channel_id=1, source_target_pairs={{0,4},{1,5},{2,6},{3,7},{4,0},{5,1},{6,2},{7,3},{8,12},{9,13},{10,... | collective-permute-start | bytes 122888 | tf_op jit(solution)/shard_map/ppermute | solution.py:186
  3.1 0.7 %xor_multiply_fusion = s32[16]{0:T(128)S(1)} fusion(s32[16]{0:T(128)} %constant.32.clone, s32[]{:T(128)S(6)} %axis_index.12), kind=kLoop, calls=%fused_computation.11 | loop fusion | flops 32 | bytes 132 | tf_op jit(solution)/shard_map/mul | solution.py:192
  4.4 0.9 %collective-permute-done = bf16[8,2560]{1,0:T(8,128)(2,1)S(1)} collective-permute-done((bf16[8,2560]{1,0:T(8,128)(2,1)}, bf16[8,2560]{1,0:T(8,128)(2,1)S(1)}, u32[]{:S(2)}, u32[]{:S(2)}) %collective-permute-start) | collective-permute-done | bytes 40992 | tf_op jit(solution)/shard_map/ppermute | solution.py:186
  5.2 0.8 %pad_maximum_fusion.3 = bf16[16,2560]{1,0:T(8,128)(2,1)S(1)} fusion(bf16[8,2560]{1,0:T(8,128)(2,1)S(1)} %collective-permute-done, bf16[8,2560]{1,0:T(8,128)(2,1)} %param.8), kind=kLoop, calls=%fused_computation.3 | loop fusion | flops 163840 | bytes 163840 | tf_op jit(solution)/shard_map/concatenate | solution.py:190
  6.0 3.0 %collective-permute-start.1 = (bf16[16,2560]{1,0:T(8,128)(2,1)S(1)}, bf16[16,2560]{1,0:T(8,128)(2,1)S(1)}, u32[]{:S(2)}, u32[]{:S(2)}) collective-permute-start(bf16[16,2560]{1,0:T(8,128)(2,1)S(1)} %pad_maximum_fusion.3), channel_id=1, source_target_pairs={{0,8},{1,9},{2,10},{3,11},{4,12},{5,13},{6,14},{7,15},{8,0},{9,1},... | collective-permute-start | bytes 245768 | tf_op jit(solution)/shard_map/ppermute | solution.py:186
  9.1 0.1 fusion.1
  9.8 0.1 reshape.47
  9.9 1.6 %collective-permute-done.1 = bf16[16,2560]{1,0:T(8,128)(2,1)S(1)} collective-permute-done((bf16[16,2560]{1,0:T(8,128)(2,1)S(1)}, bf16[16,2560]{1,0:T(8,128)(2,1)S(1)}, u32[]{:S(2)}, u32[]{:S(2)}) %collective-permute-start.1) | collective-permute-done | bytes 81952 | tf_op jit(solution)/shard_map/ppermute | solution.py:186
  11.5 1.9 %collective-permute-start.2 = (bf16[32,2560]{1,0:T(8,128)(2,1)S(1)}, bf16[32,2560]{1,0:T(8,128)(2,1)S(1)}, u32[]{:S(2)}, u32[]{:S(2)}) collective-permute-start(bf16[32,2560]{1,0:T(8,128)(2,1)S(1)} %pad_maximum_fusion.2), channel_id=1, source_target_pairs={{0,2},{1,3},{2,0},{3,1},{4,6},{5,7},{6,4},{7,5},{8,10},{9,11},{10,... | collective-permute-start | bytes 491528 | tf_op jit(solution)/shard_map/ppermute | solution.py:186
  13.4 0.1 fusion
  13.5 0.1 div.24
  13.6 3.3 %collective-permute-done.2 = bf16[32,2560]{1,0:T(8,128)(2,1)S(1)} collective-permute-done((bf16[32,2560]{1,0:T(8,128)(2,1)S(1)}, bf16[32,2560]{1,0:T(8,128)(2,1)S(1)}, u32[]{:S(2)}, u32[]{:S(2)}) %collective-permute-start.2) | collective-permute-done | bytes 163872 | tf_op jit(solution)/shard_map/ppermute | solution.py:186
  16.9 0.1 collective-permute-start.3
  17.0 1.6 %collective-permute-done.3 = bf16[64,2560]{1,0:T(8,128)(2,1)S(1)} collective-permute-done((bf16[64,2560]{1,0:T(8,128)(2,1)S(1)}, bf16[64,2560]{1,0:T(8,128)(2,1)S(1)}, u32[]{:S(2)}, u32[]{:S(2)}) %collective-permute-start.3) | collective-permute-done | bytes 327712 | tf_op jit(solution)/shard_map/ppermute | solution.py:186
  18.7 0.1 broadcast_in_dim.4.qf_ref
  18.7 0.0 copy-done.1
  18.7 0.0 copy-done
  18.8 20.8 %attend.1 = (f32[64,2560]{1,0:T(8,128)S(1)}, f32[64,128]{1,0:T(8,128)S(1)}, s16[64,2688]{1,0:T(8,128)(2,1)S(1)}) custom-call(s32[1]{0:T(128)S(6)} %min.6.limit_ref, bf16[128,2560]{1,0:T(8,128)(2,1)S(1)} %pad_maximum_fusion.q_ref, bf16[1024,2560]{1,0:T(8,128)(2,1)} %k_hbm.1, bf16[1024,2560]{1,0:T(8,128)(2,1)} %v_hbm.1, bf16[8,2560]{1,0:T(8,128)(2,1)S(1)} %copy-done, ...), custom_call_target="tpu_custom_call" | custom-call | flops 2013265920 | bytes 10485760 | tf_op jit(solution)/shard_map/attend/pallas_call | solution.py:113
  39.6 0.2 collective-permute-start.4
  39.8 1.5 %collective-permute-done.4.b_ref = s16[64,2688]{1,0:T(8,128)(2,1)S(1)} collective-permute-done((s16[64,2688]{1,0:T(8,128)(2,1)S(1)}, s16[64,2688]{1,0:T(8,128)(2,1)S(1)}, u32[]{:S(2)}, u32[]{:S(2)}) %collective-permute-start.4) | collective-permute-done | bytes 344096 | tf_op jit(solution)/shard_map/ppermute | solution.py:186
  41.3 2.0 %merge.4 = (f32[32,2560]{1,0:T(8,128)S(1)}, f32[32,128]{1,0:T(8,128)S(1)}, s16[32,2688]{1,0:T(8,128)(2,1)S(1)}) custom-call(f32[64,2560]{1,0:T(8,128)S(1)} %get-tuple-element.17.a_ref, f32[64,128]{1,0:T(8,128)S(1)} %get-tuple-element.18.a_log_ref, s16[64,2688]{1,0:T(8,128)(2,1)S(1)} %collective-permute-done.4.b_ref), custom_call_target="tpu_custom_call" | custom-call | tf_op jit(solution)/shard_map/merge/pallas_call | solution.py:159
  43.3 1.9 %collective-permute-start.5 = (s16[32,2688]{1,0:T(8,128)(2,1)S(1)}, s16[32,2688]{1,0:T(8,128)(2,1)S(1)}, u32[]{:S(2)}, u32[]{:S(2)}) collective-permute-start(s16[32,2688]{1,0:T(8,128)(2,1)S(1)} %get-tuple-element.22), channel_id=1, source_target_pairs={{0,2},{1,3},{2,0},{3,1},{4,6},{5,7},{6,4},{7,5},{8,10},{9,11},{10,... | collective-permute-start | bytes 516104 | tf_op jit(solution)/shard_map/ppermute | solution.py:186
  45.1 4.7 %collective-permute-done.5.b_ref = s16[32,2688]{1,0:T(8,128)(2,1)S(1)} collective-permute-done((s16[32,2688]{1,0:T(8,128)(2,1)S(1)}, s16[32,2688]{1,0:T(8,128)(2,1)S(1)}, u32[]{:S(2)}, u32[]{:S(2)}) %collective-permute-start.5) | collective-permute-done | bytes 172064 | tf_op jit(solution)/shard_map/ppermute | solution.py:186
  49.8 1.6 %merge.5 = (f32[16,2560]{1,0:T(8,128)S(1)}, f32[16,128]{1,0:T(8,128)S(1)}, s16[16,2688]{1,0:T(8,128)(2,1)S(1)}) custom-call(f32[32,2560]{1,0:T(8,128)S(1)} %get-tuple-element.20.a_ref, f32[32,128]{1,0:T(8,128)S(1)} %get-tuple-element.21.a_log_ref, s16[32,2688]{1,0:T(8,128)(2,1)S(1)} %collective-permute-done.5.b_ref), custom_call_target="tpu_custom_call" | custom-call | tf_op jit(solution)/shard_map/merge/pallas_call | solution.py:159
  51.5 2.9 %collective-permute-start.6 = (s16[16,2688]{1,0:T(8,128)(2,1)S(1)}, s16[16,2688]{1,0:T(8,128)(2,1)S(1)}, u32[]{:S(2)}, u32[]{:S(2)}) collective-permute-start(s16[16,2688]{1,0:T(8,128)(2,1)S(1)} %get-tuple-element.25), channel_id=1, source_target_pairs={{0,8},{1,9},{2,10},{3,11},{4,12},{5,13},{6,14},{7,15},{8,0},{9,1},... | collective-permute-start | bytes 258056 | tf_op jit(solution)/shard_map/ppermute | solution.py:186
  54.4 4.3 %collective-permute-done.6.b_ref = s16[16,2688]{1,0:T(8,128)(2,1)S(1)} collective-permute-done((s16[16,2688]{1,0:T(8,128)(2,1)S(1)}, s16[16,2688]{1,0:T(8,128)(2,1)S(1)}, u32[]{:S(2)}, u32[]{:S(2)}) %collective-permute-start.6) | collective-permute-done | bytes 86048 | tf_op jit(solution)/shard_map/ppermute | solution.py:186
  58.7 0.8 %merge.6 = (f32[8,2560]{1,0:T(8,128)S(1)}, f32[8,128]{1,0:T(8,128)S(1)}, s16[8,2688]{1,0:T(8,128)(2,1)S(1)}) custom-call(f32[16,2560]{1,0:T(8,128)S(1)} %get-tuple-element.23.a_ref, f32[16,128]{1,0:T(8,128)S(1)} %get-tuple-element.24.a_log_ref, s16[16,2688]{1,0:T(8,128)(2,1)S(1)} %collective-permute-done.6.b_ref), custom_call_target="tpu_custom_call" | custom-call | tf_op jit(solution)/shard_map/merge/pallas_call | solution.py:159
  59.5 0.4 collective-permute-start.7
  59.9 3.6 %collective-permute-done.7.b_ref = s16[8,2688]{1,0:T(8,128)(2,1)S(1)} collective-permute-done((s16[8,2688]{1,0:T(8,128)(2,1)S(1)}, s16[8,2688]{1,0:T(8,128)(2,1)S(1)}, u32[]{:S(2)}, u32[]{:S(2)}) %collective-permute-start.7) | collective-permute-done | bytes 43040 | tf_op jit(solution)/shard_map/ppermute | solution.py:186
  63.6 0.8 %merge.7 = bf16[8,2560]{1,0:T(8,128)(2,1)} custom-call(f32[8,2560]{1,0:T(8,128)S(1)} %get-tuple-element.26.a_ref, f32[8,128]{1,0:T(8,128)S(1)} %get-tuple-element.27.a_log_ref, s16[8,2688]{1,0:T(8,128)(2,1)S(1)} %collective-permute-done.7.b_ref), custom_call_target="tpu_custom_call" | custom-call | tf_op jit(solution)/shard_map/merge/pallas_call | solution.py:159
  (6 shorter events, 0.1 us)
Async XLA Ops:
  0.0 18.7 %copy-start.1 = (bf16[8,2560]{1,0:T(8,128)(2,1)S(1)}, bf16[8,2560]{1,0:T(8,128)(2,1)}, u32[]{:S(2)}) copy-start(bf16[8,2560]{1,0:T(8,128)(2,1)} %sv_ref.1) | copy-start | bytes 122884
  0.0 18.7 %copy-start = (bf16[8,2560]{1,0:T(8,128)(2,1)S(1)}, bf16[8,2560]{1,0:T(8,128)(2,1)}, u32[]{:S(2)}) copy-start(bf16[8,2560]{1,0:T(8,128)(2,1)} %sk_ref.1) | copy-start | bytes 122884
  0.0 5.2 %collective-permute-start = (bf16[8,2560]{1,0:T(8,128)(2,1)}, bf16[8,2560]{1,0:T(8,128)(2,1)S(1)}, u32[]{:S(2)}, u32[]{:S(2)}) collective-permute-start(bf16[8,2560]{1,0:T(8,128)(2,1)} %param.8), channel_id=1, source_target_pairs={{0,4},{1,5},{2,6},{3,7},{4,0},{5,1},{6,2},{7,3},{8,12},{9,13},{10,... | collective-permute-start | bytes 122888 | tf_op jit(solution)/shard_map/ppermute | solution.py:186
  6.0 5.5 %collective-permute-start.1 = (bf16[16,2560]{1,0:T(8,128)(2,1)S(1)}, bf16[16,2560]{1,0:T(8,128)(2,1)S(1)}, u32[]{:S(2)}, u32[]{:S(2)}) collective-permute-start(bf16[16,2560]{1,0:T(8,128)(2,1)S(1)} %pad_maximum_fusion.3), channel_id=1, source_target_pairs={{0,8},{1,9},{2,10},{3,11},{4,12},{5,13},{6,14},{7,15},{8,0},{9,1},... | collective-permute-start | bytes 245768 | tf_op jit(solution)/shard_map/ppermute | solution.py:186
  11.5 5.4 %collective-permute-start.2 = (bf16[32,2560]{1,0:T(8,128)(2,1)S(1)}, bf16[32,2560]{1,0:T(8,128)(2,1)S(1)}, u32[]{:S(2)}, u32[]{:S(2)}) collective-permute-start(bf16[32,2560]{1,0:T(8,128)(2,1)S(1)} %pad_maximum_fusion.2), channel_id=1, source_target_pairs={{0,2},{1,3},{2,0},{3,1},{4,6},{5,7},{6,4},{7,5},{8,10},{9,11},{10,... | collective-permute-start | bytes 491528 | tf_op jit(solution)/shard_map/ppermute | solution.py:186
  16.9 1.7 %collective-permute-start.3 = (bf16[64,2560]{1,0:T(8,128)(2,1)S(1)}, bf16[64,2560]{1,0:T(8,128)(2,1)S(1)}, u32[]{:S(2)}, u32[]{:S(2)}) collective-permute-start(bf16[64,2560]{1,0:T(8,128)(2,1)S(1)} %pad_maximum_fusion.1), channel_id=1, source_target_pairs={{0,1},{1,0},{2,3},{3,2},{4,5},{5,4},{6,7},{7,6},{8,9},{9,8},{10,11... | collective-permute-start | bytes 983048 | tf_op jit(solution)/shard_map/ppermute | solution.py:186
  39.6 1.7 %collective-permute-start.4 = (s16[64,2688]{1,0:T(8,128)(2,1)S(1)}, s16[64,2688]{1,0:T(8,128)(2,1)S(1)}, u32[]{:S(2)}, u32[]{:S(2)}) collective-permute-start(s16[64,2688]{1,0:T(8,128)(2,1)S(1)} %get-tuple-element.19), channel_id=1, source_target_pairs={{0,1},{1,0},{2,3},{3,2},{4,5},{5,4},{6,7},{7,6},{8,9},{9,8},{10,11... | collective-permute-start | bytes 1032200 | tf_op jit(solution)/shard_map/ppermute | solution.py:186
  43.3 6.6 %collective-permute-start.5 = (s16[32,2688]{1,0:T(8,128)(2,1)S(1)}, s16[32,2688]{1,0:T(8,128)(2,1)S(1)}, u32[]{:S(2)}, u32[]{:S(2)}) collective-permute-start(s16[32,2688]{1,0:T(8,128)(2,1)S(1)} %get-tuple-element.22), channel_id=1, source_target_pairs={{0,2},{1,3},{2,0},{3,1},{4,6},{5,7},{6,4},{7,5},{8,10},{9,11},{10,... | collective-permute-start | bytes 516104 | tf_op jit(solution)/shard_map/ppermute | solution.py:186
  51.5 7.3 %collective-permute-start.6 = (s16[16,2688]{1,0:T(8,128)(2,1)S(1)}, s16[16,2688]{1,0:T(8,128)(2,1)S(1)}, u32[]{:S(2)}, u32[]{:S(2)}) collective-permute-start(s16[16,2688]{1,0:T(8,128)(2,1)S(1)} %get-tuple-element.25), channel_id=1, source_target_pairs={{0,8},{1,9},{2,10},{3,11},{4,12},{5,13},{6,14},{7,15},{8,0},{9,1},... | collective-permute-start | bytes 258056 | tf_op jit(solution)/shard_map/ppermute | solution.py:186
  59.5 4.0 %collective-permute-start.7 = (s16[8,2688]{1,0:T(8,128)(2,1)S(1)}, s16[8,2688]{1,0:T(8,128)(2,1)S(1)}, u32[]{:S(2)}, u32[]{:S(2)}) collective-permute-start(s16[8,2688]{1,0:T(8,128)(2,1)S(1)} %get-tuple-element.28), channel_id=1, source_target_pairs={{0,4},{1,5},{2,6},{3,7},{4,0},{5,1},{6,2},{7,3},{8,12},{9,13},{10,... | collective-permute-start | bytes 129032 | tf_op jit(solution)/shard_map/ppermute | solution.py:186

commit v3 on v2

v3 whole, which is shorter than its diff:
```python
import functools
import math

import jax
import jax.numpy as jnp
from jax import lax
from jax.experimental import pallas as pl
from jax.experimental.pallas import tpu as pltpu
from jax.sharding import PartitionSpec as P

HEAD_DIM = 128
HEADS = 20
FRAME_TOK = 1560
LANES = 128
PART = 32
NEG_FILL = -1e30
LOG_FLOOR = -30000.0
FIXED = 32768.0
HALF_RANGE = 32768
STEPS = 32512.0
PEAK_FLOOR = 1e-30
SCALE = math.log2(math.e) / math.sqrt(HEAD_DIM)
WIDTH = HEADS * HEAD_DIM
PAIR = 2 * HEAD_DIM
BLOCK = 128
CHUNK = 128
PAD = 16
LAST = (((1,), (1,)), ((), ()))
FIRST = (((0,), (0,)), ((), ()))


def power_of(peak):
    return jnp.ceil(jnp.log2(jnp.maximum(peak, PEAK_FLOOR)))


def pack(scaled):
    return jnp.round(scaled).astype(jnp.int32).astype(jnp.int16)


def unpack(steps):
    return steps.astype(jnp.int32).astype(jnp.float32)


def pack_stats(log_sum, power):
    fixed = jnp.round(log_sum * FIXED).astype(jnp.int32)
    high = fixed // HALF_RANGE
    low = fixed - high * HALF_RANGE
    lane = lax.broadcasted_iota(jnp.int32, log_sum.shape, 1)
    packed = jnp.where(lane < PART, high, pltpu.roll(low, PART, 1))
    packed = jnp.where(lane < 2 * PART, packed, pltpu.roll(power.astype(jnp.int32), 2 * PART, 1))
    return packed.astype(jnp.int16)


def unpack_stats(packed):
    packed = packed.astype(jnp.int32)
    fixed = packed * HALF_RANGE + pltpu.roll(packed, LANES - PART, 1)
    power = pltpu.roll(packed, LANES - 2 * PART, 1)
    return fixed.astype(jnp.float32) * (1.0 / FIXED), power.astype(jnp.float32)


def attend_kernel(
    limit_ref, q_ref, k_hbm, v_hbm, sk_ref, sv_ref, qf_ref, kf_ref, keep_ref, keep_stats_ref, send_ref,
    k_ref, v_ref, sems, bias_ref, s_even, s_odd, top_ref, logs_ref, powers_ref,
):
    rows, keys, own = q_ref.shape[0], k_ref.shape[1], sk_ref.shape[0]
    half = rows // 2
    pairs = HEADS // 2
    scores = (s_even, s_odd)

    def copy_of(pair, which):
        cols = pl.ds(pl.multiple_of(pair * PAIR, PAIR), PAIR)
        source, target = ((k_hbm, k_ref), (v_hbm, v_ref))[which]
        return pltpu.make_async_copy(source.at[:, cols], target.at[pair], sems.at[pair, which])

    for pair in range(pairs):
        copy_of(pair, 0).start()
        copy_of(pair, 1).start()
    logs_ref[...] = jnp.zeros_like(logs_ref)
    powers_ref[...] = jnp.zeros_like(powers_ref)
    slot = lax.broadcasted_iota(jnp.int32, bias_ref.shape, 0)
    bias_ref[...] = jnp.where(slot < limit_ref[0], 0.0, NEG_FILL)
    pad = jnp.zeros((PAD - own, PAIR), jnp.bfloat16)

    def block_at(block):
        again = not isinstance(block, int)
        first = pl.multiple_of(block * BLOCK, BLOCK) if again else block * BLOCK
        block_rows = pl.ds(first, BLOCK)
        span_bias = jnp.where(kf_ref[...] <= qf_ref[0:1, block_rows], 0.0, NEG_FILL)
        span_bias = jnp.concatenate([span_bias, span_bias], axis=1)

        def columns(pair):
            return pl.ds(pl.multiple_of(pair * PAIR, PAIR), PAIR)

        def score(pair, slot):
            cols = columns(pair)
            q = q_ref[block_rows, cols]
            zero = jnp.zeros((BLOCK, HEAD_DIM), q.dtype)
            q = jnp.concatenate(
                [jnp.concatenate([q[:, :HEAD_DIM], zero], 1), jnp.concatenate([zero, q[:, HEAD_DIM:]], 1)], 0
            )
            s2 = lax.dot_general(sk_ref[:, cols], q, LAST, preferred_element_type=jnp.float32) + span_bias
            scores[slot][keys:, :] = s2
            tops = s2
            for chunk in range(0, keys, CHUNK):
                part = pl.ds(chunk, CHUNK)
                s = lax.dot_general(k_ref[pair, part, :], q, LAST, preferred_element_type=jnp.float32)
                bias = bias_ref[part, :]
                s = s + jnp.concatenate([bias, bias], axis=1)
                scores[slot][part, :] = s
                tops = jnp.maximum(tops, jnp.max(s.reshape(CHUNK // 8, 8, PAIR), axis=0))
                yield
            top_ref[slot : slot + 1, :] = jnp.max(tops, axis=0, keepdims=True)

        def weigh(pair, slot, beside):
            cols = columns(pair)
            sv = jnp.concatenate([sv_ref[:, cols], pad], 0)
            top = top_ref[slot : slot + 1, :]
            outs = []
            for head in range(2):
                lanes = slice(head * HEAD_DIM, (head + 1) * HEAD_DIM)
                head_top = top[:, lanes]
                total = jnp.zeros((8, HEAD_DIM), jnp.float32)
                parts = []
                for chunk in list(range(0, keys, 2 * CHUNK)) + [keys]:
                    size = 2 * CHUNK if chunk < keys else own
                    if chunk < keys:
                        next(beside, None)
                    p = jnp.exp2((scores[slot][chunk : chunk + size, lanes] - head_top) * SCALE)
                    total = total + jnp.sum(p.reshape(size // 8, 8, HEAD_DIM), axis=0)
                    high = p.astype(jnp.bfloat16)
                    low = (p - high.astype(jnp.float32)).astype(jnp.bfloat16)
                    parts.append(jnp.concatenate([high, low], axis=1))
                both = lax.dot_general(
                    v_ref[pair, :, lanes], jnp.concatenate(parts[:-1], 0), FIRST, preferred_element_type=jnp.float32
                ) + lax.dot_general(
                    sv[:, lanes], jnp.concatenate([parts[-1], pad], 0), FIRST, preferred_element_type=jnp.float32
                )
                total = jnp.sum(total, axis=0, keepdims=True)
                o = (both[:, :HEAD_DIM] + both[:, HEAD_DIM:]) * (1.0 / total)
                power = power_of(jnp.max(jnp.abs(o), axis=0, keepdims=True))
                steps = jnp.exp2(-power) * STEPS
                if rows == BLOCK:
                    lane = lax.broadcasted_iota(jnp.int32, steps.shape, 1)
                    steps = jnp.where(lane < half, 1.0, steps)
                else:
                    steps = jnp.where(first < half, 1.0, steps)
                outs.append(jnp.transpose(o * steps))
                here = pl.ds(pair * 2 + head, 1)
                logs_ref[block, here, :] = jnp.maximum(head_top * SCALE + jnp.log2(total), LOG_FLOOR)
                powers_ref[block, here, :] = power
            for _ in beside:
                pass
            o = jnp.concatenate(outs, axis=1)
            if rows == BLOCK:
                keep_ref[:, cols] = o[:half]
                send_ref[:, cols] = pack(o[half:])
            else:
                @pl.when(first < half)
                def _():
                    keep_ref[block_rows, cols] = o

                @pl.when(first >= half)
                def _():
                    send_ref[pl.ds(pl.multiple_of(first - half, BLOCK), BLOCK), cols] = pack(o)

        def arrive(pair, which):
            if not again:
                copy_of(pair, which).wait()

        arrive(0, 0)
        for _ in score(0, 0):
            pass

        @pl.loop(0, pairs // 2 - 1)
        def _(twice):
            for slot in range(2):
                pair = twice * 2 + slot
                arrive(pair, 1)
                arrive(pair + 1, 0)
                weigh(pair, slot, score(pair + 1, 1 - slot))

        arrive(pairs - 2, 1)
        arrive(pairs - 1, 0)
        weigh(pairs - 2, 0, score(pairs - 1, 1))
        arrive(pairs - 1, 1)
        weigh(pairs - 1, 1, iter(()))

    block_at(0)
    if rows > BLOCK:
        pl.loop(1, rows // BLOCK)(block_at)
    for block in range(rows // BLOCK):
        logs, powers = jnp.transpose(logs_ref[block]), jnp.transpose(powers_ref[block])
        here = slice(block * BLOCK, min((block + 1) * BLOCK, half))
        kept = max(here.stop - here.start, 0)
        if kept:
            keep_stats_ref[here, :] = join_stats(logs[:kept], powers[:kept])
        if kept < BLOCK:
            there = slice(block * BLOCK + kept - half, (block + 1) * BLOCK - half)
            send_ref[there, WIDTH:] = pack_stats(logs[kept:], powers[kept:])


def join_stats(log_sum, power):
    lane = lax.broadcasted_iota(jnp.int32, log_sum.shape, 1)
    return jnp.where(lane < PART, log_sum, pltpu.roll(power, PART, 1))


def halves(rows):
    return [
        jax.ShapeDtypeStruct((rows, WIDTH), jnp.float32),
        jax.ShapeDtypeStruct((rows, LANES), jnp.float32),
        jax.ShapeDtypeStruct((rows, WIDTH + LANES), jnp.int16),
    ]


def attend(limit, q, k, v, sk, sv, query_frame, key_frame):
    vmem = pl.BlockSpec(memory_space=pltpu.VMEM)
    hbm = pl.BlockSpec(memory_space=pltpu.HBM)
    rows, keys, own = q.shape[0], k.shape[0], sk.shape[0]
    pairs = HEADS // 2
    return pl.pallas_call(
        attend_kernel,
        in_specs=[pl.BlockSpec(memory_space=pltpu.SMEM), vmem, hbm, hbm] + [vmem] * 4,
        out_specs=[vmem] * 3,
        out_shape=halves(rows // 2),
        scratch_shapes=[
            pltpu.VMEM((pairs, keys, PAIR), k.dtype),
            pltpu.VMEM((pairs, keys, PAIR), v.dtype),
            pltpu.SemaphoreType.DMA((pairs, 2)),
            pltpu.VMEM((keys, LANES), jnp.float32),
            pltpu.VMEM((keys + own, PAIR), jnp.float32),
            pltpu.VMEM((keys + own, PAIR), jnp.float32),
            pltpu.VMEM((8, PAIR), jnp.float32),
            pltpu.VMEM((rows // BLOCK, LANES, BLOCK), jnp.float32),
            pltpu.VMEM((rows // BLOCK, LANES, BLOCK), jnp.float32),
        ],
        compiler_params=pltpu.CompilerParams(vmem_limit_bytes=50 << 20),
        cost_estimate=pl.CostEstimate(
            flops=6 * rows * keys * WIDTH, bytes_accessed=4 * keys * WIDTH, transcendentals=rows * keys * HEADS
        ),
        name="attend",
    )(limit, q, k, v, sk, sv, query_frame, key_frame)


def merge_kernel(last, a_ref, a_stats_ref, b_ref, *outs):
    a_log = a_stats_ref[...]
    a_power = pltpu.roll(a_log, LANES - PART, 1)
    b_log, b_power = unpack_stats(b_ref[:, WIDTH:])
    rows = a_log.shape[0]
    half = rows if last else rows // 2
    top = jnp.maximum(a_log, b_log)
    a_weight, b_weight = jnp.exp2(a_log - top), jnp.exp2(b_log - top)
    total = a_weight + b_weight
    a_share, b_share = a_weight / total, b_weight / total * (jnp.exp2(b_power) * (1.0 / STEPS))
    if not last:
        power = jnp.maximum(a_power, b_power)
        row = lax.broadcasted_iota(jnp.int32, power.shape, 0)
        steps = jnp.where(row < half, 1.0, jnp.exp2(-power) * STEPS)
        a_share, b_share = a_share * steps, b_share * steps
    for head in range(HEADS):
        cols = slice(head * HEAD_DIM, (head + 1) * HEAD_DIM)
        o = a_ref[:, cols] * a_share[:, head : head + 1] + unpack(b_ref[:, cols]) * b_share[:, head : head + 1]
        outs[0][:, cols] = o[:half].astype(outs[0].dtype)
        if not last:
            outs[2][:, cols] = pack(o[half:])
    if not last:
        log_sum = jnp.maximum(top + jnp.log2(total), LOG_FLOOR)
        outs[1][...] = join_stats(log_sum[:half], power[:half])
        outs[2][:, WIDTH:] = pack_stats(log_sum[half:], power[half:])


def merge(a, a_stats, b, last):
    rows = a.shape[0]
    shapes = [jax.ShapeDtypeStruct((rows, WIDTH), jnp.bfloat16)] if last else halves(rows // 2)
    vmem = pl.BlockSpec(memory_space=pltpu.VMEM)
    return pl.pallas_call(
        functools.partial(merge_kernel, last),
        in_specs=[vmem] * 3,
        out_specs=[vmem] * len(shapes),
        out_shape=shapes,
        compiler_params=pltpu.CompilerParams(vmem_limit_bytes=16 << 20),
        name="merge",
    )(a, a_stats, b)


def strides(devices):
    order = []
    stride = 2
    while stride < devices:
        order.append(stride)
        stride *= 2
    if len(order) >= 2:
        order = order[1:] + order[:1]
    return order + [1]


def local(devices, queries, cache_keys, cache_values, span_keys, span_values, cache_tokens, span_start):
    me = lax.axis_index("seq")
    cache_rows, own = cache_keys.shape[0], queries.shape[0]
    order = strides(devices)

    def swap(x, stride):
        return lax.ppermute(x, "seq", [(i, i ^ stride) for i in range(devices)])

    q, holder = queries, [0]
    for stride in order:
        q = lax.optimization_barrier(jnp.concatenate([q, swap(q, stride)], axis=0))
        holder = holder + [h ^ stride for h in holder]
    position = (me ^ jnp.array(holder, jnp.int32))[:, None] * own + jnp.arange(own, dtype=jnp.int32)[None, :]
    query_frame = (span_start[0] + position.reshape(-1)) // FRAME_TOK
    query_frame = jnp.broadcast_to(query_frame[None, :], (8, devices * own))
    key_frame = (span_start[0] + me * own + jnp.arange(own, dtype=jnp.int32)) // FRAME_TOK
    key_frame = jnp.broadcast_to(key_frame[:, None], (own, LANES))
    limit = jnp.clip(cache_tokens - me * cache_rows, 0, cache_rows)
    keep, keep_stats, send = attend(
        limit, q, cache_keys, cache_values, span_keys, span_values, query_frame, key_frame
    )
    for stride in order[:0:-1]:
        keep, keep_stats, send = merge(keep, keep_stats, swap(send, stride), False)
    return merge(keep, keep_stats, swap(send, order[0]), True)[0]


def solution(mesh):
    rows = P(("groups", "seq"), None)
    placed = (rows, rows, rows, rows, rows, P("groups"), P("groups"))
    return jax.shard_map(
        functools.partial(local, mesh.shape["seq"]), mesh=mesh, in_specs=placed, out_specs=rows, check_vma=False
    )
```

time: 64.6 us -> 50.3 us (0.78)
  Pallas kernels: 26.1 us -> 11.7 us
    pallas_call x1, Pallas kernels: 20.8 us -> 9.61 us  [attend(): pl.pallas_call(attend_kernel, in_specs=[pl.BlockSpec(memory_space=pltpu.S...]
    pallas_call x4, Pallas kernels: 5.28 us -> 2.05 us  [merge(): pl.pallas_call(functools.partial(merge_kernel, last), in_specs=[vmem] * 3...]
where the time goes in v3:
time: 50.3 us; the launch traced here: 50.1 us
  waiting for transfers between devices  21.5 us (43%)
  starting transfers between devices  13.6 us (27%)
  Pallas kernels  11.7 us (23%)
  other arithmetic  1.71 us (3%)
  between operations  1.38 us (3%)
    ppermute x8, waiting for transfers between devices, swap(): return lax.ppermute(x, 'seq', [(i, i ^ stride) for i in range(devices)])  21.5 us
    ppermute x8, starting transfers between devices, swap(): return lax.ppermute(x, 'seq', [(i, i ^ stride) for i in range(devices)])  13.6 us
    pallas_call x1, Pallas kernels, attend(): pl.pallas_call(attend_kernel, in_specs=[pl.BlockSpec(memory_space=pltpu.S...  9.61 us
    pallas_call x4, Pallas kernels, merge(): pl.pallas_call(functools.partial(merge_kernel, last), in_specs=[vmem] * 3...  2.05 us
  transfers between devices with their start and end apart: 8, of which 8 were waited for; matrix products, arithmetic and copies ran while one was open for 2% of the time, Pallas kernels for 0%

profile of v3, /device:TPU:0, one launch (start us, length us, event | category | flops | bytes accessed | tf_op | source)
XLA Modules:
  0.0 50.1 jit_solution(7431763615401401171)
XLA Ops:
  0.0 0.0 copy-start.1
  0.0 0.0 copy-start
  0.0 3.1 %collective-permute-start = (bf16[8,2560]{1,0:T(8,128)(2,1)}, bf16[8,2560]{1,0:T(8,128)(2,1)S(1)}, u32[]{:S(2)}, u32[]{:S(2)}) collective-permute-start(bf16[8,2560]{1,0:T(8,128)(2,1)} %param.8), channel_id=1, source_target_pairs={{0,4},{1,5},{2,6},{3,7},{4,0},{5,1},{6,2},{7,3},{8,12},{9,13},{10,... | collective-permute-start | bytes 122888 | tf_op jit(solution)/shard_map/ppermute | solution.py:302
  3.1 0.7 %xor_multiply_fusion = s32[16]{0:T(128)S(1)} fusion(s32[16]{0:T(128)} %constant.32.clone, s32[]{:T(128)S(6)} %axis_index.12), kind=kLoop, calls=%fused_computation.11 | loop fusion | flops 32 | bytes 132 | tf_op jit(solution)/shard_map/mul | solution.py:308
  4.4 0.9 %collective-permute-done = bf16[8,2560]{1,0:T(8,128)(2,1)S(1)} collective-permute-done((bf16[8,2560]{1,0:T(8,128)(2,1)}, bf16[8,2560]{1,0:T(8,128)(2,1)S(1)}, u32[]{:S(2)}, u32[]{:S(2)}) %collective-permute-start) | collective-permute-done | bytes 40992 | tf_op jit(solution)/shard_map/ppermute | solution.py:302
  5.2 0.8 %pad_maximum_fusion.3 = bf16[16,2560]{1,0:T(8,128)(2,1)S(1)} fusion(bf16[8,2560]{1,0:T(8,128)(2,1)S(1)} %collective-permute-done, bf16[8,2560]{1,0:T(8,128)(2,1)} %param.8), kind=kLoop, calls=%fused_computation.3 | loop fusion | flops 163840 | bytes 163840 | tf_op jit(solution)/shard_map/concatenate | solution.py:306
  6.0 3.0 %collective-permute-start.1 = (bf16[16,2560]{1,0:T(8,128)(2,1)S(1)}, bf16[16,2560]{1,0:T(8,128)(2,1)S(1)}, u32[]{:S(2)}, u32[]{:S(2)}) collective-permute-start(bf16[16,2560]{1,0:T(8,128)(2,1)S(1)} %pad_maximum_fusion.3), channel_id=1, source_target_pairs={{0,8},{1,9},{2,10},{3,11},{4,12},{5,13},{6,14},{7,15},{8,0},{9,1},... | collective-permute-start | bytes 245768 | tf_op jit(solution)/shard_map/ppermute | solution.py:302
  9.1 0.1 fusion.1
  9.8 0.1 reshape.47
  9.9 1.6 %collective-permute-done.1 = bf16[16,2560]{1,0:T(8,128)(2,1)S(1)} collective-permute-done((bf16[16,2560]{1,0:T(8,128)(2,1)S(1)}, bf16[16,2560]{1,0:T(8,128)(2,1)S(1)}, u32[]{:S(2)}, u32[]{:S(2)}) %collective-permute-start.1) | collective-permute-done | bytes 81952 | tf_op jit(solution)/shard_map/ppermute | solution.py:302
  11.5 1.9 %collective-permute-start.2 = (bf16[32,2560]{1,0:T(8,128)(2,1)S(1)}, bf16[32,2560]{1,0:T(8,128)(2,1)S(1)}, u32[]{:S(2)}, u32[]{:S(2)}) collective-permute-start(bf16[32,2560]{1,0:T(8,128)(2,1)S(1)} %pad_maximum_fusion.2), channel_id=1, source_target_pairs={{0,2},{1,3},{2,0},{3,1},{4,6},{5,7},{6,4},{7,5},{8,10},{9,11},{10,... | collective-permute-start | bytes 491528 | tf_op jit(solution)/shard_map/ppermute | solution.py:302
  13.4 0.1 fusion
  13.5 0.1 div.24
  13.6 3.3 %collective-permute-done.2 = bf16[32,2560]{1,0:T(8,128)(2,1)S(1)} collective-permute-done((bf16[32,2560]{1,0:T(8,128)(2,1)S(1)}, bf16[32,2560]{1,0:T(8,128)(2,1)S(1)}, u32[]{:S(2)}, u32[]{:S(2)}) %collective-permute-start.2) | collective-permute-done | bytes 163872 | tf_op jit(solution)/shard_map/ppermute | solution.py:302
  16.9 0.1 collective-permute-start.3
  17.0 1.6 %collective-permute-done.3 = bf16[64,2560]{1,0:T(8,128)(2,1)S(1)} collective-permute-done((bf16[64,2560]{1,0:T(8,128)(2,1)S(1)}, bf16[64,2560]{1,0:T(8,128)(2,1)S(1)}, u32[]{:S(2)}, u32[]{:S(2)}) %collective-permute-start.3) | collective-permute-done | bytes 327712 | tf_op jit(solution)/shard_map/ppermute | solution.py:302
  18.7 0.1 broadcast_in_dim.5.kf_ref
  18.7 0.0 copy-done.1
  18.7 0.0 copy-done
  18.7 9.6 %attend.1 = (f32[64,2560]{1,0:T(8,128)S(1)}, f32[64,128]{1,0:T(8,128)S(1)}, s16[64,2688]{1,0:T(8,128)(2,1)S(1)}) custom-call(s32[1]{0:T(128)S(6)} %min.6.limit_ref, bf16[128,2560]{1,0:T(8,128)(2,1)S(1)} %pad_maximum_fusion.q_ref, bf16[1024,2560]{1,0:T(8,128)(2,1)} %k_hbm.1, bf16[1024,2560]{1,0:T(8,128)(2,1)} %v_hbm.1, bf16[8,2560]{1,0:T(8,128)(2,1)S(1)} %copy-done, ...), custom_call_target="tpu_custom_call" | custom-call | flops 2013265920 | bytes 10485760 | tf_op jit(solution)/shard_map/attend/pallas_call | solution.py:220
  28.3 0.2 collective-permute-start.4
  28.5 1.5 %collective-permute-done.4.b_ref = s16[64,2688]{1,0:T(8,128)(2,1)S(1)} collective-permute-done((s16[64,2688]{1,0:T(8,128)(2,1)S(1)}, s16[64,2688]{1,0:T(8,128)(2,1)S(1)}, u32[]{:S(2)}, u32[]{:S(2)}) %collective-permute-start.4) | collective-permute-done | bytes 344096 | tf_op jit(solution)/shard_map/ppermute | solution.py:302
  30.1 0.5 %merge.4 = (f32[32,2560]{1,0:T(8,128)S(1)}, f32[32,128]{1,0:T(8,128)S(1)}, s16[32,2688]{1,0:T(8,128)(2,1)S(1)}) custom-call(f32[64,2560]{1,0:T(8,128)S(1)} %get-tuple-element.17.a_ref, f32[64,128]{1,0:T(8,128)S(1)} %get-tuple-element.18.a_stats_ref, s16[64,2688]{1,0:T(8,128)(2,1)S(1)} %collective-permute-done.4.b_ref), custom_call_target="tpu_custom_call" | custom-call | tf_op jit(solution)/shard_map/merge/pallas_call | solution.py:275
  30.6 1.9 %collective-permute-start.5 = (s16[32,2688]{1,0:T(8,128)(2,1)S(1)}, s16[32,2688]{1,0:T(8,128)(2,1)S(1)}, u32[]{:S(2)}, u32[]{:S(2)}) collective-permute-start(s16[32,2688]{1,0:T(8,128)(2,1)S(1)} %get-tuple-element.22), channel_id=1, source_target_pairs={{0,2},{1,3},{2,0},{3,1},{4,6},{5,7},{6,4},{7,5},{8,10},{9,11},{10,... | collective-permute-start | bytes 516104 | tf_op jit(solution)/shard_map/ppermute | solution.py:302
  32.5 4.7 %collective-permute-done.5.b_ref = s16[32,2688]{1,0:T(8,128)(2,1)S(1)} collective-permute-done((s16[32,2688]{1,0:T(8,128)(2,1)S(1)}, s16[32,2688]{1,0:T(8,128)(2,1)S(1)}, u32[]{:S(2)}, u32[]{:S(2)}) %collective-permute-start.5) | collective-permute-done | bytes 172064 | tf_op jit(solution)/shard_map/ppermute | solution.py:302
  37.2 0.4 merge.5
  37.6 3.0 %collective-permute-start.6 = (s16[16,2688]{1,0:T(8,128)(2,1)S(1)}, s16[16,2688]{1,0:T(8,128)(2,1)S(1)}, u32[]{:S(2)}, u32[]{:S(2)}) collective-permute-start(s16[16,2688]{1,0:T(8,128)(2,1)S(1)} %get-tuple-element.25), channel_id=1, source_target_pairs={{0,8},{1,9},{2,10},{3,11},{4,12},{5,13},{6,14},{7,15},{8,0},{9,1},... | collective-permute-start | bytes 258056 | tf_op jit(solution)/shard_map/ppermute | solution.py:302
  40.5 4.3 %collective-permute-done.6.b_ref = s16[16,2688]{1,0:T(8,128)(2,1)S(1)} collective-permute-done((s16[16,2688]{1,0:T(8,128)(2,1)S(1)}, s16[16,2688]{1,0:T(8,128)(2,1)S(1)}, u32[]{:S(2)}, u32[]{:S(2)}) %collective-permute-start.6) | collective-permute-done | bytes 86048 | tf_op jit(solution)/shard_map/ppermute | solution.py:302
  44.9 0.3 merge.6
  45.2 0.5 collective-permute-start.7
  45.6 3.6 %collective-permute-done.7.b_ref = s16[8,2688]{1,0:T(8,128)(2,1)S(1)} collective-permute-done((s16[8,2688]{1,0:T(8,128)(2,1)S(1)}, s16[8,2688]{1,0:T(8,128)(2,1)S(1)}, u32[]{:S(2)}, u32[]{:S(2)}) %collective-permute-start.7) | collective-permute-done | bytes 43040 | tf_op jit(solution)/shard_map/ppermute | solution.py:302
  49.3 0.8 %merge.7 = bf16[8,2560]{1,0:T(8,128)(2,1)} custom-call(f32[8,2560]{1,0:T(8,128)S(1)} %get-tuple-element.26.a_ref, f32[8,128]{1,0:T(8,128)S(1)} %get-tuple-element.27.a_stats_ref, s16[8,2688]{1,0:T(8,128)(2,1)S(1)} %collective-permute-done.7.b_ref), custom_call_target="tpu_custom_call" | custom-call | tf_op jit(solution)/shard_map/merge/pallas_call | solution.py:275
  (6 shorter events, 0.1 us)
Async XLA Ops:
  0.0 18.7 %copy-start.1 = (bf16[8,2560]{1,0:T(8,128)(2,1)S(1)}, bf16[8,2560]{1,0:T(8,128)(2,1)}, u32[]{:S(2)}) copy-start(bf16[8,2560]{1,0:T(8,128)(2,1)} %sv_ref.1) | copy-start | bytes 122884
  0.0 18.7 %copy-start = (bf16[8,2560]{1,0:T(8,128)(2,1)S(1)}, bf16[8,2560]{1,0:T(8,128)(2,1)}, u32[]{:S(2)}) copy-start(bf16[8,2560]{1,0:T(8,128)(2,1)} %sk_ref.1) | copy-start | bytes 122884
  0.0 5.2 %collective-permute-start = (bf16[8,2560]{1,0:T(8,128)(2,1)}, bf16[8,2560]{1,0:T(8,128)(2,1)S(1)}, u32[]{:S(2)}, u32[]{:S(2)}) collective-permute-start(bf16[8,2560]{1,0:T(8,128)(2,1)} %param.8), channel_id=1, source_target_pairs={{0,4},{1,5},{2,6},{3,7},{4,0},{5,1},{6,2},{7,3},{8,12},{9,13},{10,... | collective-permute-start | bytes 122888 | tf_op jit(solution)/shard_map/ppermute | solution.py:302
  6.0 5.5 %collective-permute-start.1 = (bf16[16,2560]{1,0:T(8,128)(2,1)S(1)}, bf16[16,2560]{1,0:T(8,128)(2,1)S(1)}, u32[]{:S(2)}, u32[]{:S(2)}) collective-permute-start(bf16[16,2560]{1,0:T(8,128)(2,1)S(1)} %pad_maximum_fusion.3), channel_id=1, source_target_pairs={{0,8},{1,9},{2,10},{3,11},{4,12},{5,13},{6,14},{7,15},{8,0},{9,1},... | collective-permute-start | bytes 245768 | tf_op jit(solution)/shard_map/ppermute | solution.py:302
  11.5 5.4 %collective-permute-start.2 = (bf16[32,2560]{1,0:T(8,128)(2,1)S(1)}, bf16[32,2560]{1,0:T(8,128)(2,1)S(1)}, u32[]{:S(2)}, u32[]{:S(2)}) collective-permute-start(bf16[32,2560]{1,0:T(8,128)(2,1)S(1)} %pad_maximum_fusion.2), channel_id=1, source_target_pairs={{0,2},{1,3},{2,0},{3,1},{4,6},{5,7},{6,4},{7,5},{8,10},{9,11},{10,... | collective-permute-start | bytes 491528 | tf_op jit(solution)/shard_map/ppermute | solution.py:302
  16.9 1.7 %collective-permute-start.3 = (bf16[64,2560]{1,0:T(8,128)(2,1)S(1)}, bf16[64,2560]{1,0:T(8,128)(2,1)S(1)}, u32[]{:S(2)}, u32[]{:S(2)}) collective-permute-start(bf16[64,2560]{1,0:T(8,128)(2,1)S(1)} %pad_maximum_fusion.1), channel_id=1, source_target_pairs={{0,1},{1,0},{2,3},{3,2},{4,5},{5,4},{6,7},{7,6},{8,9},{9,8},{10,11... | collective-permute-start | bytes 983048 | tf_op jit(solution)/shard_map/ppermute | solution.py:302
  28.3 1.7 %collective-permute-start.4 = (s16[64,2688]{1,0:T(8,128)(2,1)S(1)}, s16[64,2688]{1,0:T(8,128)(2,1)S(1)}, u32[]{:S(2)}, u32[]{:S(2)}) collective-permute-start(s16[64,2688]{1,0:T(8,128)(2,1)S(1)} %get-tuple-element.19), channel_id=1, source_target_pairs={{0,1},{1,0},{2,3},{3,2},{4,5},{5,4},{6,7},{7,6},{8,9},{9,8},{10,11... | collective-permute-start | bytes 1032200 | tf_op jit(solution)/shard_map/ppermute | solution.py:302
  30.6 6.6 %collective-permute-start.5 = (s16[32,2688]{1,0:T(8,128)(2,1)S(1)}, s16[32,2688]{1,0:T(8,128)(2,1)S(1)}, u32[]{:S(2)}, u32[]{:S(2)}) collective-permute-start(s16[32,2688]{1,0:T(8,128)(2,1)S(1)} %get-tuple-element.22), channel_id=1, source_target_pairs={{0,2},{1,3},{2,0},{3,1},{4,6},{5,7},{6,4},{7,5},{8,10},{9,11},{10,... | collective-permute-start | bytes 516104 | tf_op jit(solution)/shard_map/ppermute | solution.py:302
  37.6 7.3 %collective-permute-start.6 = (s16[16,2688]{1,0:T(8,128)(2,1)S(1)}, s16[16,2688]{1,0:T(8,128)(2,1)S(1)}, u32[]{:S(2)}, u32[]{:S(2)}) collective-permute-start(s16[16,2688]{1,0:T(8,128)(2,1)S(1)} %get-tuple-element.25), channel_id=1, source_target_pairs={{0,8},{1,9},{2,10},{3,11},{4,12},{5,13},{6,14},{7,15},{8,0},{9,1},... | collective-permute-start | bytes 258056 | tf_op jit(solution)/shard_map/ppermute | solution.py:302
  45.2 4.1 %collective-permute-start.7 = (s16[8,2688]{1,0:T(8,128)(2,1)S(1)}, s16[8,2688]{1,0:T(8,128)(2,1)S(1)}, u32[]{:S(2)}, u32[]{:S(2)}) collective-permute-start(s16[8,2688]{1,0:T(8,128)(2,1)S(1)} %get-tuple-element.28), channel_id=1, source_target_pairs={{0,4},{1,5},{2,6},{3,7},{4,0},{5,1},{6,2},{7,3},{8,12},{9,13},{10,... | collective-permute-start | bytes 129032 | tf_op jit(solution)/shard_map/ppermute | solution.py:302
